TPU v7x, 32 devices: a whole 2x2x4 slice. The times are simulated.
32 devices in a mesh: fsdp: 8 (over z, y), tp: 4 (over x, core).
Axes of the slice: x: 2, y: 2, z: 4, core: 2. Of those that a mesh axis runs over, the one named last changes fastest.
Arguments:
- inputs: bfloat16 [16, 736, 1152], P('fsdp', 'tp'), may hold values from -6 to 6
- cotangent: bfloat16 [16, 736, 1152], P('fsdp', 'tp'), may hold values from -6 to 6
- lengths: int32 [16], P('fsdp'), may hold values from 1 to 729, as said below
- ln1_gain: bfloat16 [1152], P('fsdp'), may hold values from 0.099609375 to 1.8984375
- ln1_bias: bfloat16 [1152], P('fsdp'), may hold values from -0.3125 to 0.3125
- q_weight: bfloat16 [1152, 1152], P('fsdp', 'tp'), may hold values from -0.1875 to 0.1875
- q_bias: bfloat16 [1152], P('tp'), may hold values from -3 to 3
- k_weight: bfloat16 [1152, 1152], P('fsdp', 'tp'), may hold values from -0.1875 to 0.1875
- v_weight: bfloat16 [1152, 1152], P('fsdp', 'tp'), may hold values from -0.1875 to 0.1875
- v_bias: bfloat16 [1152], P('tp'), may hold values from -0.1875 to 0.1875
- out_weight: bfloat16 [1152, 1152], P('tp', 'fsdp'), may hold values from -2.5 to 2.5
- out_bias: bfloat16 [1152], P('fsdp'), may hold values from -1.75 to 1.75
- ln2_gain: bfloat16 [1152], P('fsdp'), may hold values from 0.099609375 to 1.8984375
- ln2_bias: bfloat16 [1152], P('fsdp'), may hold values from -1.75 to 1.75
- up_weight: bfloat16 [1152, 4304], P('fsdp', 'tp'), may hold values from -0.1875 to 0.1875
- up_bias: bfloat16 [4304], P('tp'), may hold values from -1.75 to 1.75
- down_weight: bfloat16 [4304, 1152], P('tp', 'fsdp'), may hold values from -0.09375 to 0.09375
- down_bias: bfloat16 [1152], P('fsdp'), may hold values from -1.75 to 1.75
Outputs:
- layer_out: bfloat16 [16, 736, 1152], P('fsdp', 'tp')
- input_grad: float32 [16, 736, 1152], P('fsdp', 'tp')
- ln1_gain_grad: float32 [1152], P('fsdp')
- ln1_bias_grad: float32 [1152], P('fsdp')
- q_weight_grad: float32 [1152, 1152], P('fsdp', 'tp')
- q_bias_grad: float32 [1152], P('tp')
- k_weight_grad: float32 [1152, 1152], P('fsdp', 'tp')
- v_weight_grad: float32 [1152, 1152], P('fsdp', 'tp')
- v_bias_grad: float32 [1152], P('tp')
- out_weight_grad: float32 [1152, 1152], P('tp', 'fsdp')
- out_bias_grad: float32 [1152], P('fsdp')
- ln2_gain_grad: float32 [1152], P('fsdp')
- ln2_bias_grad: float32 [1152], P('fsdp')
- up_weight_grad: float32 [1152, 4304], P('fsdp', 'tp')
- up_bias_grad: float32 [4304], P('tp')
- down_weight_grad: float32 [4304, 1152], P('tp', 'fsdp')
- down_bias_grad: float32 [1152], P('fsdp')
Inputs may be any that keep to these rules, and one draw needn't show every extreme that they name: `lengths`: each slot either holds one image of 729 tokens or is empty with length 1; exactly 11 slots hold images, which ones drawn from the seed.
All inputs are finite; a program needn't handle non-finite values.
Results may differ from a plain program's by a relative error of at most 0.013.
Values may be sent and summed in bfloat16 or wider, within the bound.
No kernel may reach another device: no remote copies, remote signals or barrier semaphores. Data moves between devices by JAX's collectives and lax.ppermute only.
A program may use at most 192 MiB of HBM per device.

v0:
```python
import jax
import jax.numpy as jnp
from jax import lax
from jax.sharding import PartitionSpec as P

HD = 72


epsilon = 1e-06
negative_big = -1e30


def layer_norm(row_block, gain_vec, shift_vec):
    average = jnp.mean(row_block, -1, keepdims=True)
    center = row_block - average
    variance = jnp.mean(center * center, -1, keepdims=True)
    return center * lax.rsqrt(variance + epsilon) * gain_vec + shift_vec


def gelu_tanh(values_in):
    return jax.nn.gelu(values_in, approximate=True)


def plain_dot(left, right):
    return jnp.dot(left, right, preferred_element_type=jnp.float32)


def contract_rows(left, right):
    return lax.dot_general(
        left, right, (((0,), (0,)), ((), ())), preferred_element_type=jnp.float32
    )


def contract_cols(left, right):
    return lax.dot_general(
        left, right, (((1,), (1,)), ((), ())), preferred_element_type=jnp.float32
    )


def local(
    inputs,
    cotangent,
    lengths,
    ln1_gain,
    ln1_bias,
    q_weight,
    q_bias,
    k_weight,
    v_weight,
    v_bias,
    out_weight,
    out_bias,
    ln2_gain,
    ln2_bias,
    up_weight,
    up_bias,
    down_weight,
    down_bias,
):
    tp_count = lax.axis_size("tp")
    tp_index = lax.axis_index("tp")
    fsdp_index = lax.axis_index("fsdp")
    micro_count = inputs.shape[0]
    local_rows = inputs.shape[1]
    model_width = inputs.shape[2]
    seq_len = local_rows * tp_count
    head_width = q_weight.shape[1]
    heads_here = head_width // HD
    unit_width = up_weight.shape[1]
    scale_value = HD ** (-0.5)
    q_shift = q_bias.astype(jnp.float32)
    v_shift = v_bias.astype(jnp.float32)
    up_shift = up_bias.astype(jnp.float32)

    def fetch_weights():
        attn_full = (
            lax.all_gather(ln1_gain, "fsdp", axis=0, tiled=True),
            lax.all_gather(ln1_bias, "fsdp", axis=0, tiled=True),
            lax.all_gather(q_weight, "fsdp", axis=0, tiled=True),
            lax.all_gather(k_weight, "fsdp", axis=0, tiled=True),
            lax.all_gather(v_weight, "fsdp", axis=0, tiled=True),
            lax.all_gather(out_weight, "fsdp", axis=1, tiled=True),
            lax.all_gather(out_bias, "fsdp", axis=0, tiled=True),
        )
        mlp_full = (
            lax.all_gather(ln2_gain, "fsdp", axis=0, tiled=True),
            lax.all_gather(ln2_bias, "fsdp", axis=0, tiled=True),
            lax.all_gather(up_weight, "fsdp", axis=0, tiled=True),
            lax.all_gather(down_weight, "fsdp", axis=1, tiled=True),
            lax.all_gather(down_bias, "fsdp", axis=0, tiled=True),
        )
        return (attn_full, mlp_full)

    def masked_scores(queries, keys_all, key_valid):
        query_heads = queries.reshape(seq_len, heads_here, HD)
        key_heads = keys_all.reshape(seq_len, heads_here, HD)
        scores = (
            jnp.einsum("qhd,khd->hqk", query_heads, key_heads, preferred_element_type=jnp.float32)
            * scale_value
        )
        return jnp.where(key_valid[None, None, :], scores, negative_big)

    def forward(slot_rows, length, attn_full, mlp_full):
        gain_one, shift_one, wq_full, wk_full, wv_full, wo_full, bo_full = attn_full
        gain_two, shift_two, w_up, w_down, bd_full = mlp_full
        key_valid = jnp.arange(seq_len, dtype=jnp.int32) < length
        norm_one = layer_norm(
            slot_rows, gain_one.astype(jnp.float32), shift_one.astype(jnp.float32)
        ).astype(jnp.bfloat16)
        norm_full = lax.all_gather(norm_one, "tp", axis=0, tiled=True)
        queries = (plain_dot(norm_full, wq_full) + q_shift).astype(jnp.bfloat16)
        keys_all = plain_dot(norm_full, wk_full).astype(jnp.bfloat16)
        values_all = (plain_dot(norm_full, wv_full) + v_shift).astype(jnp.bfloat16)
        scores = masked_scores(queries, keys_all, key_valid)
        row_max = jnp.max(scores, -1, keepdims=True)
        row_total = jnp.sum(jnp.exp(scores - row_max), -1, keepdims=True)
        log_total = row_max + jnp.log(row_total)
        soft_low = jnp.exp(scores - log_total).astype(jnp.bfloat16)
        value_heads = values_all.reshape(seq_len, heads_here, HD)
        mixed_heads = jnp.einsum(
            "hqk,khd->qhd", soft_low, value_heads, preferred_element_type=jnp.float32
        )
        mixed_heads = mixed_heads.astype(jnp.bfloat16).reshape(seq_len, head_width)
        attended = lax.psum_scatter(
            plain_dot(mixed_heads, wo_full), "tp", scatter_dimension=0, tiled=True
        )
        middle = slot_rows + attended + bo_full.astype(jnp.float32)
        norm_two = layer_norm(
            middle, gain_two.astype(jnp.float32), shift_two.astype(jnp.float32)
        ).astype(jnp.bfloat16)
        norm_two_full = lax.all_gather(norm_two, "tp", axis=0, tiled=True)
        hidden = plain_dot(norm_two_full, w_up) + up_shift
        active = gelu_tanh(hidden).astype(jnp.bfloat16)
        mlp_rows = lax.psum_scatter(
            plain_dot(active, w_down), "tp", scatter_dimension=0, tiled=True
        )
        out_rows = middle + mlp_rows + bd_full.astype(jnp.float32)
        kept_state = (
            norm_full,
            queries,
            keys_all,
            values_all,
            log_total,
            mixed_heads,
            middle,
            norm_two_full,
            hidden,
            active,
        )
        return (out_rows, kept_state)

    outputs = []
    for slot_index in range(micro_count):
        attn_full, mlp_full = fetch_weights()
        out_rows, kept_state = forward(
            inputs[slot_index].astype(jnp.float32), lengths[slot_index], attn_full, mlp_full
        )
        outputs.append(out_rows.astype(jnp.bfloat16))
    grad_list = []
    totals = None
    for slot_index in range(micro_count):
        attn_full, mlp_full = fetch_weights()
        slot_rows = inputs[slot_index].astype(jnp.float32)
        kept_state = forward(slot_rows, lengths[slot_index], attn_full, mlp_full)[1]
        backward_length = lengths[slot_index]
        (
            backward_gain_one,
            backward_shift_one,
            backward_wq_full,
            backward_wk_full,
            backward_wv_full,
            backward_wo_full,
            backward_bo_full,
        ) = attn_full
        backward_gain_two, backward_shift_two, backward_w_up, backward_w_down, backward_bd_full = (
            mlp_full
        )
        (
            backward_norm_full,
            backward_queries,
            backward_keys_all,
            backward_values_all,
            backward_log_total,
            backward_mixed_heads,
            backward_middle,
            backward_norm_two_full,
            backward_hidden,
            backward_active,
        ) = kept_state
        backward_key_valid = jnp.arange(seq_len, dtype=jnp.int32) < backward_length
        row_valid = (
            jnp.arange(local_rows, dtype=jnp.int32) + tp_index * local_rows < backward_length
        ).astype(jnp.float32)
        grad_out = cotangent[slot_index].astype(jnp.float32) * row_valid[:, None]
        backward_down_sum = jnp.sum(grad_out, 0)
        grad_out_full = lax.all_gather(grad_out.astype(jnp.bfloat16), "tp", axis=0, tiled=True)
        backward_grad_w_down = contract_rows(backward_active, grad_out_full)
        grad_active = contract_cols(grad_out_full, backward_w_down)
        gelu_pull = jax.vjp(gelu_tanh, backward_hidden)[1]
        grad_hidden = gelu_pull(grad_active)[0].astype(jnp.bfloat16)
        backward_up_sum = jnp.sum(grad_hidden.astype(jnp.float32), 0)
        backward_grad_w_up = contract_rows(backward_norm_two_full, grad_hidden)
        grad_norm_two = lax.psum_scatter(
            contract_cols(grad_hidden, backward_w_up), "tp", scatter_dimension=0, tiled=True
        )
        norm_two_pull = jax.vjp(
            layer_norm,
            backward_middle,
            backward_gain_two.astype(jnp.float32),
            backward_shift_two.astype(jnp.float32),
        )[1]
        middle_part, backward_gain_two_grad, backward_shift_two_grad = norm_two_pull(grad_norm_two)
        grad_middle = grad_out + middle_part
        backward_out_sum = jnp.sum(grad_middle, 0)
        grad_middle_full = lax.all_gather(
            grad_middle.astype(jnp.bfloat16), "tp", axis=0, tiled=True
        )
        backward_grad_w_out = contract_rows(backward_mixed_heads, grad_middle_full)
        grad_mixed = (
            contract_cols(grad_middle_full, backward_wo_full)
            .astype(jnp.bfloat16)
            .reshape(seq_len, heads_here, HD)
        )
        soft_weights = jnp.exp(
            masked_scores(backward_queries, backward_keys_all, backward_key_valid)
            - backward_log_total
        )
        backward_soft_low = soft_weights.astype(jnp.bfloat16)
        backward_query_heads = backward_queries.reshape(seq_len, heads_here, HD)
        backward_key_heads = backward_keys_all.reshape(seq_len, heads_here, HD)
        backward_value_heads = backward_values_all.reshape(seq_len, heads_here, HD)
        grad_soft = jnp.einsum(
            "qhd,khd->hqk", grad_mixed, backward_value_heads, preferred_element_type=jnp.float32
        )
        row_inner = jnp.sum(soft_weights * grad_soft, -1, keepdims=True)
        grad_scores = (soft_weights * (grad_soft - row_inner)).astype(jnp.bfloat16)
        grad_queries = (
            (
                jnp.einsum(
                    "hqk,khd->qhd",
                    grad_scores,
                    backward_key_heads,
                    preferred_element_type=jnp.float32,
                )
                * scale_value
            )
            .astype(jnp.bfloat16)
            .reshape(seq_len, head_width)
        )
        grad_keys = (
            (
                jnp.einsum(
                    "hqk,qhd->khd",
                    grad_scores,
                    backward_query_heads,
                    preferred_element_type=jnp.float32,
                )
                * scale_value
            )
            .astype(jnp.bfloat16)
            .reshape(seq_len, head_width)
        )
        grad_values = (
            jnp.einsum(
                "hqk,qhd->khd", backward_soft_low, grad_mixed, preferred_element_type=jnp.float32
            )
            .astype(jnp.bfloat16)
            .reshape(seq_len, head_width)
        )
        backward_query_sum = jnp.sum(grad_queries.astype(jnp.float32), 0)
        backward_value_sum = jnp.sum(grad_values.astype(jnp.float32), 0)
        backward_grad_wq = contract_rows(backward_norm_full, grad_queries)
        backward_grad_wk = contract_rows(backward_norm_full, grad_keys)
        backward_grad_wv = contract_rows(backward_norm_full, grad_values)
        part_q = contract_cols(grad_queries, backward_wq_full)
        part_k = contract_cols(grad_keys, backward_wk_full)
        part_v = contract_cols(grad_values, backward_wv_full)
        grad_norm_one = lax.psum_scatter(
            part_q + part_k + part_v, "tp", scatter_dimension=0, tiled=True
        )
        norm_one_pull = jax.vjp(
            layer_norm,
            slot_rows,
            backward_gain_one.astype(jnp.float32),
            backward_shift_one.astype(jnp.float32),
        )[1]
        rows_part, backward_gain_one_grad, backward_shift_one_grad = norm_one_pull(grad_norm_one)
        grad_rows = grad_middle + rows_part
        slot_grads = (
            backward_gain_one_grad,
            backward_shift_one_grad,
            backward_grad_wq,
            backward_query_sum,
            backward_grad_wk,
            backward_grad_wv,
            backward_value_sum,
            backward_grad_w_out,
            backward_out_sum,
            backward_gain_two_grad,
            backward_shift_two_grad,
            backward_grad_w_up,
            backward_up_sum,
            backward_grad_w_down,
            backward_down_sum,
        )
        grad_rows, slot_grads = (grad_rows, slot_grads)
        grad_list.append(grad_rows)
        if totals is None:
            totals = slot_grads
        else:
            totals = jax.tree.map(jnp.add, totals, slot_grads)
    (
        gain_one_grad,
        shift_one_grad,
        grad_wq,
        query_sum,
        grad_wk,
        grad_wv,
        value_sum,
        grad_w_out,
        out_sum,
        gain_two_grad,
        shift_two_grad,
        grad_w_up,
        up_sum,
        grad_w_down,
        down_sum,
    ) = totals
    summed_weights = (
        lax.psum_scatter(grad_wq, "fsdp", scatter_dimension=0, tiled=True),
        lax.psum_scatter(grad_wk, "fsdp", scatter_dimension=0, tiled=True),
        lax.psum_scatter(grad_wv, "fsdp", scatter_dimension=0, tiled=True),
        lax.psum_scatter(grad_w_out, "fsdp", scatter_dimension=1, tiled=True),
        lax.psum_scatter(grad_w_up, "fsdp", scatter_dimension=0, tiled=True),
        lax.psum_scatter(grad_w_down, "fsdp", scatter_dimension=1, tiled=True),
    )
    width_stack = jnp.stack(
        [gain_one_grad, shift_one_grad, out_sum, gain_two_grad, shift_two_grad, down_sum], 0
    )
    head_stack = jnp.zeros((2, head_width * tp_count), jnp.float32)
    head_stack = lax.dynamic_update_slice_in_dim(
        head_stack, jnp.stack([query_sum, value_sum], 0), tp_index * head_width, 1
    )
    unit_line = jnp.zeros((unit_width * tp_count,), jnp.float32)
    unit_line = lax.dynamic_update_slice_in_dim(unit_line, up_sum, tp_index * unit_width, 0)
    summed_small = lax.psum((width_stack, head_stack, unit_line), ("fsdp", "tp"))
    shard_size = model_width // lax.axis_size("fsdp")
    width_pieces = lax.dynamic_slice_in_dim(summed_small[0], fsdp_index * shard_size, shard_size, 1)
    head_pieces = lax.dynamic_slice_in_dim(summed_small[1], tp_index * head_width, head_width, 1)
    unit_piece = lax.dynamic_slice_in_dim(summed_small[2], tp_index * unit_width, unit_width, 0)
    return (
        jnp.stack(outputs, 0),
        jnp.stack(grad_list, 0),
        width_pieces[0],
        width_pieces[1],
        summed_weights[0],
        head_pieces[0],
        summed_weights[1],
        summed_weights[2],
        head_pieces[1],
        summed_weights[3],
        width_pieces[2],
        width_pieces[3],
        width_pieces[4],
        summed_weights[4],
        unit_piece,
        summed_weights[5],
        width_pieces[5],
    )


def solution(mesh):
    in_specs = (
        P("fsdp", "tp", None),
        P("fsdp", "tp", None),
        P("fsdp"),
        P("fsdp"),
        P("fsdp"),
        P("fsdp", "tp"),
        P("tp"),
        P("fsdp", "tp"),
        P("fsdp", "tp"),
        P("tp"),
        P("tp", "fsdp"),
        P("fsdp"),
        P("fsdp"),
        P("fsdp"),
        P("fsdp", "tp"),
        P("tp"),
        P("tp", "fsdp"),
        P("fsdp"),
    )
    out_specs = (
        P("fsdp", "tp", None),
        P("fsdp", "tp", None),
        P("fsdp"),
        P("fsdp"),
        P("fsdp", "tp"),
        P("tp"),
        P("fsdp", "tp"),
        P("fsdp", "tp"),
        P("tp"),
        P("tp", "fsdp"),
        P("fsdp"),
        P("fsdp"),
        P("fsdp"),
        P("fsdp", "tp"),
        P("tp"),
        P("tp", "fsdp"),
        P("fsdp"),
    )
    return jax.shard_map(local, mesh=mesh, in_specs=in_specs, out_specs=out_specs, check_vma=False)
```

profile of v0, /device:TPU:0, one launch (start us, length us, event | category | flops | bytes accessed | tf_op | source)
XLA Modules:
  0.0 1294.0 jit_solution(5558494795576318744)
XLA Ops:
  14.4 38.8 %all-reduce.15 = (bf16[1152]{0:T(1024)(128)(2,1)S(1)}, bf16[1152]{0:T(1024)(128)(2,1)S(1)}, bf16[1152]{0:T(1024)(128)(2,1)S(1)}, bf16[1152]{0:T(1024)(128)(2,1)S...) all-reduce(bf16[1152]{0:T(1024)(128)(2,1)S(1)} %dynamic-update-slic, ...), channel_id=1, replica_groups=mesh['fsdp'=8,'tp'=4] {'fsdp'}, use_global_device_ids=true, to_apply=%add.1 | all-reduce | flops 6912 | bytes 27648
  60.0 32.5 %all_gather.44 = bf16[1152,288]{1,0:T(8,128)(2,1)S(1)} all-gather(bf16[144,288]{1,0:T(8,128)(2,1)S(1)} %copy-done.54), channel_id=1, replica_groups=mesh['fsdp'=8,'tp'=4] {'fsdp'}, dimensions={0}, use_global_device_ids=true | all-gather | bytes 746496 | tf_op jit(solution)/shard_map/all_gather | solution.py:79
  92.5 32.2 %all_gather.45 = bf16[1152,288]{1,0:T(8,128)(2,1)S(1)} all-gather(bf16[144,288]{1,0:T(8,128)(2,1)S(1)} %copy-done.55), channel_id=1, replica_groups=mesh['fsdp'=8,'tp'=4] {'fsdp'}, dimensions={0}, use_global_device_ids=true | all-gather | bytes 746496 | tf_op jit(solution)/shard_map/all_gather | solution.py:80
  126.1 34.5 %all_gather.43 = bf16[1152,288]{1,0:T(8,128)(2,1)} all-gather(bf16[144,288]{1,0:T(8,128)(2,1)S(1)} %copy-done.56), channel_id=1, replica_groups=mesh['fsdp'=8,'tp'=4] {'fsdp'}, dimensions={0}, use_global_device_ids=true | all-gather | bytes 746496 | tf_op jit(solution)/shard_map/all_gather | solution.py:81
  160.6 32.0 %all_gather.46 = bf16[288,1152]{0,1:T(8,128)(2,1)S(1)} all-gather(bf16[288,144]{0,1:T(8,128)(2,1)S(1)} %copy-done.57), channel_id=1, replica_groups=mesh['fsdp'=8,'tp'=4] {'fsdp'}, dimensions={1}, use_global_device_ids=true | all-gather | bytes 746496 | tf_op jit(solution)/shard_map/all_gather | solution.py:82
  231.9 15.0 %reduce-scatter.47.cloned.1.call-done = f32[184,1152]{1,0:T(8,128)} async-done(((f32[736,1152]{1,0:T(8,128)}), f32[184,1152]{1,0:T(8,128)}) %reduce-scatter.47.cloned.1.call-update) | async-done | bytes 847888
  247.0 42.0 %reduce-scatter.43.cloned.1.call-done = f32[184,1152]{1,0:T(8,128)} async-done(((f32[736,1152]{1,0:T(8,128)}), f32[184,1152]{1,0:T(8,128)}) %reduce-scatter.43.cloned.1.call-update) | async-done | bytes 847888
  294.4 17.0 %all-gather.23.cloned.1.call-done = bf16[736,1152]{1,0:T(8,128)(2,1)} async-done(((bf16[184,1152]{1,0:T(8,128)(2,1)}), bf16[736,1152]{1,0:T(8,128)(2,1)}) %all-gather.23.cloned.1.call-update) | async-done | bytes 1695760 | tf_op jit(solution)/shard_map/all_gather | solution.py:196
  311.4 57.1 %all-gather.17.cloned.1.call-done = bf16[1076,1152]{0,1:T(8,128)(2,1)} async-done(((bf16[1076,144]{0,1:T(8,128)(2,1)}), bf16[1076,1152]{0,1:T(8,128)(2,1)}) %all-gather.17.cloned.1.call-update) | async-done | bytes 2479120 | tf_op jit(solution)/shard_map/all_gather | solution.py:89
  374.9 49.4 %all-gather.15.cloned.1.call-done = bf16[1152,1076]{1,0:T(8,128)(2,1)} async-done(((bf16[144,1076]{1,0:T(8,128)(2,1)}), bf16[1152,1076]{1,0:T(8,128)(2,1)}) %all-gather.15.cloned.1.call-update) | async-done | bytes 2479120 | tf_op jit(solution)/shard_map/all_gather | solution.py:88
  424.3 20.5 %all-gather.13.cloned.1.call-done = bf16[736,1152]{1,0:T(8,128)(2,1)} async-done(((bf16[184,1152]{1,0:T(8,128)(2,1)}), bf16[736,1152]{1,0:T(8,128)(2,1)}) %all-gather.13.cloned.1.call-update) | async-done | bytes 1695760 | tf_op jit(solution)/shard_map/all_gather | solution.py:131
  473.1 15.4 %all-gather.21.cloned.1.call-done = bf16[736,1152]{1,0:T(8,128)(2,1)} async-done(((bf16[184,1152]{1,0:T(8,128)(2,1)}), bf16[736,1152]{1,0:T(8,128)(2,1)}) %all-gather.21.cloned.1.call-update) | async-done | bytes 1695760 | tf_op jit(solution)/shard_map/all_gather | solution.py:131
  520.2 10.4 reduce-scatter.51.cloned.1.call-done
  530.6 42.1 %reduce-scatter.55.cloned.1.call-done = f32[184,1152]{1,0:T(8,128)} async-done(((f32[736,1152]{1,0:T(8,128)}), f32[184,1152]{1,0:T(8,128)}) %reduce-scatter.55.cloned.1.call-update) | async-done | bytes 847888
  574.8 39.9 %reduce-scatter.45.cloned.1.call-done = f32[184,1152]{1,0:T(8,128)} async-done(((f32[736,1152]{1,0:T(8,128)}), f32[184,1152]{1,0:T(8,128)}) %reduce-scatter.45.cloned.1.call-update) | async-done | bytes 847888
  614.7 42.1 %reduce-scatter.49.cloned.1.call-done = f32[184,1152]{1,0:T(8,128)} async-done(((f32[736,1152]{1,0:T(8,128)}), f32[184,1152]{1,0:T(8,128)}) %reduce-scatter.49.cloned.1.call-update) | async-done | bytes 847888
  665.4 19.5 %all-gather.29.cloned.1.call-done = bf16[736,1152]{1,0:T(8,128)(2,1)} async-done(((bf16[184,1152]{1,0:T(8,128)(2,1)}), bf16[736,1152]{1,0:T(8,128)(2,1)}) %all-gather.29.cloned.1.call-update) | async-done | bytes 1695760 | tf_op jit(solution)/shard_map/all_gather | solution.py:215
  796.5 43.7 %all-reduce.14 = (f32[6,1152]{1,0:T(8,128)}, f32[2,1152]{1,0:T(2,128)S(1)}, f32[4304]{0:T(1024)S(1)}) all-reduce(f32[6,1152]{1,0:T(8,128)S(1)} %stack.38, f32[2,1152]{1,0:T(2,128)S(1)} %dynamic_update_slice.6, f32[4304]{0:T(1024)S(1)} %add_dynamic-update-slice_fusion), channel_id=1, replica_groups=mesh['fsdp'=8,'tp'=4] {'fsdp','tp'}, use_global_device_ids=true, to_apply=%region_42.43 | all-reduce | flops 13520 | bytes 108160 | tf_op jit(solution)/shard_map/psum | solution.py:346
  848.7 52.2 %reduce-scatter.39.cloned.1.call-done = f32[144,1076]{1,0:T(8,128)} async-done(((f32[1152,1076]{1,0:T(8,128)}), f32[144,1076]{1,0:T(8,128)}) %reduce-scatter.39.cloned.1.call-update) | async-done | bytes 619792 | tf_op jit(solution)/shard_map/reduce_scatter | solution.py:334
  901.0 108.4 %reduce-scatter.41.cloned.1.call-done = f32[1076,144]{0,1:T(8,128)} async-done(((f32[1076,1152]{0,1:T(8,128)}), f32[1076,144]{0,1:T(8,128)}) %reduce-scatter.41.cloned.1.call-update) | async-done | bytes 619792 | tf_op jit(solution)/shard_map/reduce_scatter | solution.py:335
  1009.4 69.9 %reduce-scatter.37.cloned.1.call-done = f32[288,144]{0,1:T(8,128)} async-done(((f32[288,1152]{0,1:T(8,128)}), f32[288,144]{0,1:T(8,128)}) %reduce-scatter.37.cloned.1.call-update) | async-done | bytes 165904 | tf_op jit(solution)/shard_map/reduce_scatter | solution.py:333
  1079.3 69.5 %reduce-scatter.35.cloned.1.call-done = f32[144,288]{1,0:T(8,128)} async-done(((f32[1152,288]{1,0:T(8,128)}), f32[144,288]{1,0:T(8,128)}) %reduce-scatter.35.cloned.1.call-update) | async-done | bytes 165904 | tf_op jit(solution)/shard_map/reduce_scatter | solution.py:332
  1148.7 69.0 %reduce-scatter.33.cloned.1.call-done = f32[144,288]{1,0:T(8,128)} async-done(((f32[1152,288]{1,0:T(8,128)}), f32[144,288]{1,0:T(8,128)}) %reduce-scatter.33.cloned.1.call-update) | async-done | bytes 165904 | tf_op jit(solution)/shard_map/reduce_scatter | solution.py:331
  1217.7 69.0 %reduce-scatter.31.cloned.1.call-done = f32[144,288]{1,0:T(8,128)} async-done(((f32[1152,288]{1,0:T(8,128)}), f32[144,288]{1,0:T(8,128)}) %reduce-scatter.31.cloned.1.call-update) | async-done | bytes 165904 | tf_op jit(solution)/shard_map/reduce_scatter | solution.py:330
  (425 shorter events, 254.7 us)
Async XLA Ops:
  7.2 185.3 %all-gather.19.cloned.1.call-start = ((), (), s32[]{:S(2)}) async-start(), calls=%async_computation.18 | async-start | bytes 2119680 | tf_op jit(solution)/shard_map/all_gather | solution.py:110
  59.2 151.7 %all-gather.11.cloned.1.call-start = ((), (), s32[]{:S(2)}) async-start(), calls=%async_computation.14 | async-start | bytes 2119680 | tf_op jit(solution)/shard_map/all_gather | solution.py:110
  60.0 187.0 %reduce-scatter.47.cloned.1.call-start = ((), (), s32[]{:S(2)}) async-start(), calls=%async_computation.32 | async-start | bytes 4239360
  209.9 79.2 %reduce-scatter.43.cloned.1.call-start = ((), (), s32[]{:S(2)}) async-start(), calls=%async_computation.30 | async-start | bytes 4239360
  227.8 83.6 %all-gather.23.cloned.1.call-start = ((), (), s32[]{:S(2)}) async-start(), calls=%async_computation.20 | async-start | bytes 2119680 | tf_op jit(solution)/shard_map/all_gather | solution.py:196
  230.5 138.0 %all-gather.17.cloned.1.call-start = ((), (), s32[]{:S(2)}) async-start(), calls=%async_computation.17 | async-start | bytes 2985984 | tf_op jit(solution)/shard_map/all_gather | solution.py:89
  231.1 193.2 %all-gather.15.cloned.1.call-start = ((), (), s32[]{:S(2)}) async-start(), calls=%async_computation.16 | async-start | bytes 2985984 | tf_op jit(solution)/shard_map/all_gather | solution.py:88
  231.8 213.0 %all-gather.13.cloned.1.call-start = ((), (), s32[]{:S(2)}) async-start(), calls=%async_computation.15 | async-start | bytes 2119680 | tf_op jit(solution)/shard_map/all_gather | solution.py:131
  292.6 174.2 %all-gather.27.cloned.1.call-start = ((), (), s32[]{:S(2)}) async-start(), calls=%async_computation.22 | async-start | bytes 2119680 | tf_op jit(solution)/shard_map/all_gather | solution.py:196
  293.3 195.2 %all-gather.21.cloned.1.call-start = ((), (), s32[]{:S(2)}) async-start(), calls=%async_computation.19 | async-start | bytes 2119680 | tf_op jit(solution)/shard_map/all_gather | solution.py:131
  293.9 236.7 %reduce-scatter.51.cloned.1.call-start = ((), (), s32[]{:S(2)}) async-start(), calls=%async_computation.34 | async-start | bytes 4239360
  460.8 111.9 %reduce-scatter.55.cloned.1.call-start = ((), (), s32[]{:S(2)}) async-start(), calls=%async_computation.36 | async-start | bytes 4239360
  504.3 110.3 %reduce-scatter.45.cloned.1.call-start = ((), (), s32[]{:S(2)}) async-start(), calls=%async_computation.31 | async-start | bytes 4239360
  512.4 144.3 %reduce-scatter.49.cloned.1.call-start = ((), (), s32[]{:S(2)}) async-start(), calls=%async_computation.33 | async-start | bytes 4239360
  520.1 164.7 %all-gather.29.cloned.1.call-start = ((), (), s32[]{:S(2)}) async-start(), calls=%async_computation.23 | async-start | bytes 2119680 | tf_op jit(solution)/shard_map/all_gather | solution.py:215
  664.4 45.6 %all-gather.25.cloned.1.call-start = ((), (), s32[]{:S(2)}) async-start(), calls=%async_computation.21 | async-start | bytes 2119680 | tf_op jit(solution)/shard_map/all_gather | solution.py:215
  665.0 117.2 %reduce-scatter.57.cloned.1.call-start = ((), (), s32[]{:S(2)}) async-start(), calls=%async_computation.37 | async-start | bytes 4239360
  709.8 81.7 %reduce-scatter.53.cloned.1.call-start = ((), (), s32[]{:S(2)}) async-start(), calls=%async_computation.35 | async-start | bytes 4239360
  734.7 166.2 %reduce-scatter.39.cloned.1.call-start = ((), (), s32[]{:S(2)}) async-start(), calls=%async_computation.28 | async-start | bytes 5971968 | tf_op jit(solution)/shard_map/reduce_scatter | solution.py:334
  745.5 263.9 %reduce-scatter.41.cloned.1.call-start = ((), (), s32[]{:S(2)}) async-start(), calls=%async_computation.29 | async-start | bytes 5971968 | tf_op jit(solution)/shard_map/reduce_scatter | solution.py:335
  756.8 322.4 %reduce-scatter.37.cloned.1.call-start = ((), (), s32[]{:S(2)}) async-start(), calls=%async_computation.27 | async-start | bytes 1990656 | tf_op jit(solution)/shard_map/reduce_scatter | solution.py:333
  763.1 385.7 %reduce-scatter.35.cloned.1.call-start = ((), (), s32[]{:S(2)}) async-start(), calls=%async_computation.26 | async-start | bytes 1990656 | tf_op jit(solution)/shard_map/reduce_scatter | solution.py:332
  768.3 449.4 %reduce-scatter.33.cloned.1.call-start = ((), (), s32[]{:S(2)}) async-start(), calls=%async_computation.25 | async-start | bytes 1990656 | tf_op jit(solution)/shard_map/reduce_scatter | solution.py:331
  773.5 513.2 %reduce-scatter.31.cloned.1.call-start = ((), (), s32[]{:S(2)}) async-start(), calls=%async_computation.24 | async-start | bytes 1990656 | tf_op jit(solution)/shard_map/reduce_scatter | solution.py:330
  (114 other events, 1805.3 us)
Sparse Core Ops, SparseCore 0:
  59.3 17.5 all-gather.18
  79.0 20.3 all-gather.10
  210.0 36.9 reduce-scatter.46
  249.5 39.4 reduce-scatter.42
  291.0 20.3 all-gather.22
  313.4 55.0 all-gather.16
  370.6 53.5 all-gather.14
  425.8 18.9 all-gather.12
  446.4 20.3 all-gather.26
  468.1 20.3 all-gather.20
  491.1 39.4 reduce-scatter.50
  533.1 39.4 reduce-scatter.54
  575.2 39.4 reduce-scatter.44
  617.2 39.4 reduce-scatter.48
  664.5 20.3 all-gather.28
  686.3 20.3 all-gather.24
  709.9 39.4 reduce-scatter.56
  752.0 39.4 reduce-scatter.52
  795.6 105.2 reduce-scatter.38
  905.4 103.9 reduce-scatter.40
  1013.4 65.7 reduce-scatter.36
  1083.7 64.9 reduce-scatter.34
  1152.8 64.8 reduce-scatter.32
  1222.0 64.6 reduce-scatter.30
where the time goes:
time: 1300 us; the launch traced here: 1290 us
  waiting for transfers between devices  827 us (64%)
  blocking collectives  214 us (16%)
  matrix products  156 us (12%)
  other arithmetic  50 us (4%)
  local copies, waits for them, and re-layouts  26.7 us (2%)
  between operations  17.3 us (1%)
    unnamed x32, waiting for transfers between devices  205 us
    reduce_scatter x1, waiting for transfers between devices, local(): lax.psum_scatter(grad_w_down, 'fsdp', scatter_dimension=1, tiled=True)  108 us
    reduce_scatter x1, waiting for transfers between devices, local(): lax.psum_scatter(grad_w_out, 'fsdp', scatter_dimension=1, tiled=True)  69.9 us
    reduce_scatter x1, waiting for transfers between devices, local(): lax.psum_scatter(grad_wv, 'fsdp', scatter_dimension=0, tiled=True)  69.5 us
    reduce_scatter x1, waiting for transfers between devices, local(): lax.psum_scatter(grad_wq, 'fsdp', scatter_dimension=0, tiled=True)  69 us
    reduce_scatter x1, waiting for transfers between devices, local(): lax.psum_scatter(grad_wk, 'fsdp', scatter_dimension=0, tiled=True)  69 us
    all_gather x1, waiting for transfers between devices, fetch_weights(): lax.all_gather(down_weight, 'fsdp', axis=1, tiled=True)  57.1 us
    reduce_scatter x1, waiting for transfers between devices, local(): lax.psum_scatter(grad_w_up, 'fsdp', scatter_dimension=0, tiled=True)  52.2 us
  transfers between devices with their start and end apart: 24, of which 20 were waited for; matrix products, arithmetic and copies ran while one was open for 15% of the time, Pallas kernels for 0%

commit v1 on v0

v1 whole, which is shorter than its diff:
```python
import jax
import jax.numpy as jnp
from jax import lax
from jax.sharding import PartitionSpec as P

HD = 72
EPS = 1e-06
NEG = -1e30
BF = jnp.bfloat16
F32 = jnp.float32


def normalize(rows):
    average = jnp.mean(rows, -1, keepdims=True)
    center = rows - average
    variance = jnp.mean(center * center, -1, keepdims=True)
    inverse = lax.rsqrt(variance + EPS)
    return center * inverse, inverse


def norm_back(hat, inverse, gain, grad):
    scaled = grad * gain
    first = jnp.mean(scaled, -1, keepdims=True)
    second = jnp.mean(scaled * hat, -1, keepdims=True)
    return inverse * (scaled - first - hat * second)


def gelu_pair(v):
    c = 0.7978845608028654
    t = jnp.tanh(c * (v + 0.044715 * v * v * v))
    value = 0.5 * v * (1.0 + t)
    slope = 0.5 * (1.0 + t) + 0.5 * v * (1.0 - t * t) * (c * (1.0 + 3.0 * 0.044715 * v * v))
    return value, slope


def dot_nn(a, b):
    return lax.dot_general(a, b, (((1,), (0,)), ((), ())), preferred_element_type=F32)


def dot_nt(a, b):
    return lax.dot_general(a, b, (((1,), (1,)), ((), ())), preferred_element_type=F32)


def dot_tn(a, b):
    return lax.dot_general(a, b, (((0,), (0,)), ((), ())), preferred_element_type=F32)


def local(
    inputs,
    cotangent,
    lengths,
    ln1_gain,
    ln1_bias,
    q_weight,
    q_bias,
    k_weight,
    v_weight,
    v_bias,
    out_weight,
    out_bias,
    ln2_gain,
    ln2_bias,
    up_weight,
    up_bias,
    down_weight,
    down_bias,
):
    tp = lax.axis_size("tp")
    fs = lax.axis_size("fsdp")
    ti = lax.axis_index("tp")
    fi = lax.axis_index("fsdp")
    slots, rows, width = inputs.shape
    seq = rows * tp
    hw = q_weight.shape[1]
    units = up_weight.shape[1]
    heads = hw // HD
    scale = HD ** (-0.5)

    def swap_tp(x, k):
        return lax.ppermute(x, "tp", [(i, i ^ k) for i in range(tp)])

    def swap_fs(x, k):
        return lax.ppermute(x, "fsdp", [(i, i ^ k) for i in range(fs)])

    def gather_blocks(a):
        far = swap_tp(a, 2)
        near = swap_tp(jnp.stack([a, far], 0), 1)
        return jnp.concatenate([a, near[0], far, near[1]], 0)

    def block(a, j):
        return a[j * rows : (j + 1) * rows]

    def pair_sum(partial):
        other = swap_tp(
            jnp.concatenate([block(partial, 1), block(partial, 3)], 0).astype(BF), 1
        )
        mine = jnp.concatenate([block(partial, 0), block(partial, 2)], 0)
        return mine + other.astype(F32)

    def full_sum(partial):
        chip = pair_sum(partial).astype(BF)
        turned = jnp.concatenate([block(chip, 1), block(chip, 0)], 0)
        return chip.astype(F32) + swap_tp(turned, 2).astype(F32)

    def own_sum(partial):
        chip = pair_sum(partial)
        return block(chip, 0) + swap_tp(block(chip, 1).astype(BF), 2).astype(F32)

    def spread(half):
        near = swap_tp(half, 1)
        return jnp.concatenate([block(half, 0), block(near, 0), block(half, 1), block(near, 1)], 0)

    x_full = [gather_blocks(inputs[s]) for s in range(slots)]
    c_full = [gather_blocks(cotangent[s]) for s in range(slots)]

    small = jnp.stack([ln1_gain, ln1_bias, out_bias, ln2_gain, ln2_bias, down_bias, ln1_gain, ln1_gain], 0)
    small = lax.all_gather(small, "fsdp", axis=0)
    small = small.transpose(1, 0, 2).reshape(8, width).astype(F32)
    g1, b1, bo, g2, b2, bd = (small[i] for i in range(6))
    w_attn = jnp.concatenate([q_weight, k_weight, v_weight, out_weight.T], 1)
    w_attn = lax.all_gather(w_attn, "fsdp", axis=0, tiled=True)
    w_qkv = w_attn[:, : 3 * hw]
    wo_t = w_attn[:, 3 * hw :]
    pad = (-units) % 128
    w_mlp = jnp.concatenate(
        [jnp.pad(up_weight, ((0, 0), (0, pad))), jnp.pad(down_weight.T, ((0, 0), (0, pad)))], 1
    )
    w_mlp = lax.all_gather(w_mlp, "fsdp", axis=0, tiled=True)
    w_up = w_mlp[:, :units]
    wd_t = w_mlp[:, units + pad : 2 * units + pad]

    qkv_shift = jnp.concatenate([q_bias, jnp.zeros_like(q_bias), v_bias], 0).astype(F32)
    up_shift = up_bias.astype(F32)
    place = (
        (jnp.arange(tp, dtype=jnp.int32)[:, None] ^ ti) * rows
        + jnp.arange(rows, dtype=jnp.int32)[None, :]
    ).reshape(seq)

    def split_heads(a):
        return a.reshape(seq, heads, HD)

    outs, grads_x = [], []
    g_attn = g_mlp = None
    wide = head_sums = unit_sums = None
    for s in range(slots):
        valid = place < lengths[s]
        x = x_full[s].astype(F32)
        hat1, _ = normalize(x)
        n1 = (hat1 * g1 + b1).astype(BF)
        qkv = (dot_nn(n1, w_qkv) + qkv_shift).astype(BF)
        q, k, v = (split_heads(qkv[:, i * hw : (i + 1) * hw]) for i in range(3))
        scores = jnp.einsum("qhd,khd->hqk", q, k, preferred_element_type=F32) * scale
        scores = jnp.where(valid[None, None, :], scores, NEG)
        top = jnp.max(scores, -1, keepdims=True)
        lse = top + jnp.log(jnp.sum(jnp.exp(scores - top), -1, keepdims=True))
        probs = jnp.exp(scores - lse)
        probs_low = probs.astype(BF)
        mixed = jnp.einsum("hqk,khd->qhd", probs_low, v, preferred_element_type=F32)
        mixed = mixed.astype(BF).reshape(seq, hw)
        attended = full_sum(dot_nt(mixed, wo_t))
        x_half = jnp.concatenate([block(x, 0), block(x, 2)], 0)
        middle = x_half + attended + bo
        hat2, inv2 = normalize(middle)
        n2 = spread((hat2 * g2 + b2).astype(BF))
        hidden = dot_nn(n2, w_up) + up_shift
        value, slope = gelu_pair(hidden)
        active = value.astype(BF)
        outs.append((block(middle, 0) + own_sum(dot_nt(active, wd_t)) + bd).astype(BF))
        go = jnp.where(valid[:, None], c_full[s], jnp.zeros((), BF))
        g_down = dot_tn(go, active)
        gh = (dot_nn(go, wd_t) * slope).astype(BF)
        g_up = dot_tn(n2, gh)
        gn2 = full_sum(dot_nt(gh, w_up))
        go_half = jnp.concatenate([block(go, 0), block(go, 2)], 0).astype(F32)
        gm = go_half + norm_back(hat2, inv2, g2, gn2)
        gml = spread(gm.astype(BF))
        g_out = dot_tn(gml, mixed)
        gmix = split_heads(dot_nn(gml, wo_t).astype(BF))
        gp = jnp.einsum("qhd,khd->hqk", gmix, v, preferred_element_type=F32)
        inner = jnp.sum(probs * gp, -1, keepdims=True)
        gs = (probs * (gp - inner)).astype(BF)
        gq = (jnp.einsum("hqk,khd->qhd", gs, k, preferred_element_type=F32) * scale).astype(BF)
        gk = (jnp.einsum("hqk,qhd->khd", gs, q, preferred_element_type=F32) * scale).astype(BF)
        gv = jnp.einsum("hqk,qhd->khd", probs_low, gmix, preferred_element_type=F32).astype(BF)
        gqkv = jnp.concatenate([a.reshape(seq, hw) for a in (gq, gk, gv)], 1)
        g_qkv = dot_tn(n1, gqkv)
        gn1 = own_sum(dot_nt(gqkv, w_qkv))
        hat_own, inv_own = normalize(block(x, 0))
        grads_x.append(block(gm, 0) + norm_back(hat_own, inv_own, g1, gn1))
        gn2_own, hat2_own = block(gn2, 0), block(hat2, 0)
        wide_s = jnp.stack(
            [
                jnp.sum(hat_own * gn1, 0),
                jnp.sum(gn1, 0),
                jnp.sum(block(gm, 0), 0),
                jnp.sum(hat2_own * gn2_own, 0),
                jnp.sum(gn2_own, 0),
                jnp.sum(block(go_half, 0), 0),
            ],
            0,
        )
        col = jnp.sum(gqkv.astype(F32), 0)
        hs = jnp.stack([col[:hw], col[2 * hw :]], 0)
        us = jnp.sum(gh.astype(F32), 0)
        ga = jnp.concatenate([g_qkv, g_out], 1)
        gmm = (g_up, g_down)
        if s == 0:
            g_attn, g_mlp, wide, head_sums, unit_sums = ga, gmm, wide_s, hs, us
        else:
            g_attn = g_attn + ga
            g_mlp = (g_mlp[0] + gmm[0], g_mlp[1] + gmm[1])
            wide = wide + wide_s
            head_sums = head_sums + hs
            unit_sums = unit_sums + us
    gm_pack = jnp.concatenate([jnp.pad(a.astype(BF), ((0, 0), (0, pad))) for a in g_mlp], 1)
    r_mlp = lax.psum_scatter(gm_pack, "fsdp", scatter_dimension=0, tiled=True).astype(F32)
    r_attn = lax.psum_scatter(g_attn.astype(BF), "fsdp", scatter_dimension=0, tiled=True).astype(F32)

    wide = wide + swap_tp(wide, 1)
    wide = wide + swap_tp(wide, 2)
    line = jnp.concatenate([wide.reshape(-1), head_sums.reshape(-1), unit_sums], 0)
    step = 1
    while step < fs:
        line = line + swap_fs(line, step)
        step *= 2
    wide = line[: 6 * width].reshape(6, width)
    shard = width // fs
    wide = lax.dynamic_slice_in_dim(wide, fi * shard, shard, 1)
    head_sums = line[6 * width : 6 * width + 2 * hw].reshape(2, hw)
    unit_sums = line[6 * width + 2 * hw :]
    return (
        jnp.stack(outs, 0),
        jnp.stack(grads_x, 0),
        wide[0],
        wide[1],
        r_attn[:, :hw],
        head_sums[0],
        r_attn[:, hw : 2 * hw],
        r_attn[:, 2 * hw : 3 * hw],
        head_sums[1],
        r_attn[:, 3 * hw :].T,
        wide[2],
        wide[3],
        wide[4],
        r_mlp[:, :units],
        unit_sums,
        r_mlp[:, units + pad : 2 * units + pad].T,
        wide[5],
    )


def solution(mesh):
    rowed = P("fsdp", "tp", None)
    wide = P("fsdp")
    cols = P("fsdp", "tp")
    turned = P("tp", "fsdp")
    part = P("tp")
    in_specs = (
        rowed, rowed, wide, wide, wide, cols, part, cols, cols, part, turned, wide,
        wide, wide, cols, part, turned, wide,
    )
    out_specs = (
        rowed, rowed, wide, wide, cols, part, cols, cols, part, turned, wide, wide, wide,
        cols, part, turned, wide,
    )
    return jax.shard_map(local, mesh=mesh, in_specs=in_specs, out_specs=out_specs, check_vma=False)
```

time: 1300 us -> 508 us (0.39)
  waiting for transfers between devices: 827 us -> 175 us
  blocking collectives: 214 us -> 31.5 us
  local copies, waits for them, and re-layouts: 26.7 us -> 79.9 us
  matrix products: 156 us -> 108 us
  starting transfers between devices: 3.12 us -> 22.3 us
  other arithmetic: 50 us -> 67.2 us
    reduce_scatter x6 -> x0, waiting for transfers between devices: 438 us -> none  [the longest x1 108 us: local(): lax.psum_scatter(grad_w_down, 'fsdp', scatter_dimension=1, tiled=True)]
    all_gather x10 -> x2, waiting for transfers between devices: 185 us -> 0.02 us  [the longest x1 0.02 us: local(): w_attn = lax.all_gather(w_attn, 'fsdp', axis=0, tiled=True)]
    unnamed x32 -> x6, waiting for transfers between devices: 205 us -> 67 us
    ppermute x0 -> x33, waiting for transfers between devices: none -> 108 us  [the longest x30 95 us: swap_tp(): return lax.ppermute(x, 'tp', [(i, i ^ k) for i in range(tp)])]
    all_gather x4 -> x1, blocking collectives: 131 us -> 31.5 us  [local(): small = lax.all_gather(small, 'fsdp', axis=0)]
    dot_general x48 -> x36, matrix products: 156 us -> 108 us  [the longest x8 34 us: dot_nn(): lax.dot_general(a, b, (((1,), (0,)), ((), ())), preferred_element_type=F32)]
    psum x1 -> x0, blocking collectives: 43.7 us -> none  [local(): lax.psum((width_stack, head_stack, unit_line), ('fsdp', 'tp'))]
    unnamed x1 -> x0, blocking collectives: 38.8 us -> none
  transfers between devices with their start and end apart: 24 -> 37, of which waited for: 20 -> 15; matrix products, arithmetic and copies ran while one was open for 15% -> 42% of each run, Pallas kernels for 0% -> 0%
where the time goes in v1:
time: 508 us; the launch traced here: 501 us
  waiting for transfers between devices  175 us (34%)
  matrix products  108 us (21%)
  local copies, waits for them, and re-layouts  79.9 us (16%)
  other arithmetic  67.2 us (13%)
  blocking collectives  31.5 us (6%)
  starting transfers between devices  22.3 us (4%)
  between operations  16.7 us (3%)
    ppermute x30, waiting for transfers between devices, swap_tp(): return lax.ppermute(x, 'tp', [(i, i ^ k) for i in range(tp)])  95 us
    unnamed x6, waiting for transfers between devices  67 us
    unnamed x300, local copies, waits for them, and re-layouts  36.8 us
    dot_general x8, matrix products, dot_nn(): lax.dot_general(a, b, (((1,), (0,)), ((), ())), preferred_element_type=F32)  34 us
    all_gather x1, blocking collectives, local(): small = lax.all_gather(small, 'fsdp', axis=0)  31.5 us
    dot_general x8, matrix products, dot_tn(): lax.dot_general(a, b, (((0,), (0,)), ((), ())), preferred_element_type=F32)  25.3 us
    dot_general x8, matrix products, dot_nt(): lax.dot_general(a, b, (((1,), (1,)), ((), ())), preferred_element_type=F32)  25.3 us
    ppermute x30, starting transfers between devices, swap_tp(): return lax.ppermute(x, 'tp', [(i, i ^ k) for i in range(tp)])  20.4 us
  transfers between devices with their start and end apart: 37, of which 15 were waited for; matrix products, arithmetic and copies ran while one was open for 42% of the time, Pallas kernels for 0%

profile of v1, /device:TPU:0, one launch (start us, length us, event | category | flops | bytes accessed | tf_op | source)
XLA Modules:
  0.0 500.9 jit_solution(5304650829607540764)
XLA Ops:
  22.0 31.5 %all-gather = bf16[64,144]{1,0:T(8,128)(2,1)S(1)} all-gather(bf16[8,144]{1,0:T(8,128)(2,1)S(1)} %stack.133), channel_id=2, replica_groups=mesh['fsdp'=8,'tp'=4] {'fsdp'}, dimensions={0}, use_global_device_ids=true | all-gather | bytes 20736 | tf_op jit(solution)/shard_map/all_gather | solution.py:117
  65.6 3.6 maximum_select_fusion
  74.9 5.7 %add_convert_fusion.3 = bf16[736,864]{1,0:T(8,128)(2,1)S(1)} fusion(bf16[1152,1152]{1,0:T(8,128)(2,1)} %all-gather.4.cloned.1.call-done, f32[864]{0:T(1024)S(1)} %maximum_convert_fusion.2, f32[1152]{0:T(1024)S(1)} %add.336, f32[1152]{0:T(1024)S(1)} %mul.338, f32[736]{0:T(1024)S(1)} %add_rsqrt_fusion.1, f32[736]{0:T(1024)S(1)} %broadcast_multiply_fusion.1, ...), kind=kOutput, calls=%fused_computation.58 | convolution fusion | flops 1477416960 | bytes 5050496 | tf_op jit(solution)/shard_map/dot_general | solution.py:37
  88.4 4.3 add_convert_fusion.2
  132.8 17.5 %collective-permute-done.10 = bf16[368,1152]{1,0:T(8,128)(2,1)S(1)} collective-permute-done((bf16[368,1152]{1,0:T(8,128)(2,1)S(1)}, bf16[368,1152]{1,0:T(8,128)(2,1)S(1)}, u32[]{:S(2)}, u32[]{:S(2)}) %collective-permute-start.10) | collective-permute-done | bytes 847904 | tf_op jit(solution)/shard_map/ppermute | solution.py:80
  150.3 17.3 %collective-permute-done.3 = bf16[368,1152]{1,0:T(8,128)(2,1)S(1)} collective-permute-done((bf16[368,1152]{1,0:T(8,128)(2,1)S(1)}, bf16[368,1152]{1,0:T(8,128)(2,1)S(1)}, u32[]{:S(2)}, u32[]{:S(2)}) %collective-permute-start.3) | collective-permute-done | bytes 847904 | tf_op jit(solution)/shard_map/ppermute | solution.py:80
  174.7 4.9 convolution_add_fusion.3
  179.7 5.4 %convert_reduce_fusion.1 = (f32[1076]{0:T(1024)S(1)}, bf16[736,1076]{0,1:T(8,128)(2,1)S(1)}) fusion(f32[736,1076]{0,1:T(8,128)S(1)} %convolution_add_fusion.3, bf16[736,1152]{1,0:T(8,128)(2,1)S(1)} %copy-done.46, bf16[1152,2304]{1,0:T(8,128)(2,1)S(1)} %copy-done.121), kind=kOutput, calls=%fused_computation.52 | convolution fusion | flops 1841250176 | bytes 9255888 | tf_op jit(solution)/shard_map/dot_general | solution.py:37
  190.6 5.1 %convert_reduce_fusion = (f32[1076]{0:T(1024)S(1)}, bf16[736,1076]{0,1:T(8,128)(2,1)S(1)}) fusion(f32[736,1076]{0,1:T(8,128)S(1)} %convolution_add_fusion.2, bf16[736,1152]{1,0:T(8,128)(2,1)S(1)} %copy-done.43, bf16[1152,2304]{1,0:T(8,128)(2,1)S(1)} %copy-done.121), kind=kOutput, calls=%fused_computation.51 | convolution fusion | flops 1841250176 | bytes 9255888 | tf_op jit(solution)/shard_map/dot_general | solution.py:37
  204.2 5.0 fusion.142
  210.1 13.1 %collective-permute-done.24 = bf16[368,1152]{1,0:T(8,128)(2,1)S(1)} collective-permute-done((bf16[368,1152]{1,0:T(8,128)(2,1)S(1)}, bf16[368,1152]{1,0:T(8,128)(2,1)S(1)}, u32[]{:S(2)}, u32[]{:S(2)}) %collective-permute-start.24) | collective-permute-done | bytes 847904 | tf_op jit(solution)/shard_map/ppermute | solution.py:80
  223.3 17.4 %collective-permute-done.17 = bf16[368,1152]{1,0:T(8,128)(2,1)S(1)} collective-permute-done((bf16[368,1152]{1,0:T(8,128)(2,1)S(1)}, bf16[368,1152]{1,0:T(8,128)(2,1)S(1)}, u32[]{:S(2)}, u32[]{:S(2)}) %collective-permute-start.17) | collective-permute-done | bytes 847904 | tf_op jit(solution)/shard_map/ppermute | solution.py:80
  287.8 4.1 fusion.84
  292.0 4.1 fusion.85
  296.2 5.3 %fusion.7 = bf16[1152,1152]{0,1:T(8,128)(2,1)} fusion(f32[1152,288]{0,1:T(8,128)S(1)} %copy-done.83, f32[1152,864]{0,1:T(8,128)} %fusion.85, f32[1152,288]{0,1:T(8,128)S(1)} %copy-done.82, f32[1152,864]{0,1:T(8,128)} %fusion.84), kind=kLoop, calls=%fused_computation.22 | loop fusion | flops 5308416 | bytes 13271040 | tf_op jit(solution)/shard_map/convert_element_type | solution.py:217
  301.5 5.2 %copy.109 = bf16[1152,1152]{1,0:T(8,128)(2,1)} copy(bf16[1152,1152]{0,1:T(8,128)(2,1)} %fusion.7) | data formatting | bytes 5308416
  307.0 4.5 fusion.71
  322.5 8.8 %copy.111 = bf16[1152,2304]{1,0:T(8,128)(2,1)} copy(bf16[1152,2304]{0,1:T(8,128)(2,1)} %fusion.6) | data formatting | bytes 10616832
  331.3 7.8 %fusion.141 = (bf16[736,1152]{1,0:T(8,128)(2,1)S(1)}, f32[736,1152]{1,0:T(8,128)}) fusion(bf16[1152,2304]{1,0:T(8,128)(2,1)} %all-gather.6.cloned.1.call-done, f32[736,1076]{0,1:T(8,128)} %copy-done.128), kind=kOutput, calls=%fused_computation.320 | convolution fusion | flops 1832595840 | bytes 11059200 | tf_op jit(solution)/shard_map/dot_general | solution.py:41
  362.1 14.2 %collective-permute-done.20 = bf16[184,1152]{1,0:T(8,128)(2,1)S(1)} collective-permute-done((bf16[184,1152]{1,0:T(8,128)(2,1)S(1)}, bf16[184,1152]{1,0:T(8,128)(2,1)S(1)}, u32[]{:S(2)}, u32[]{:S(2)}) %collective-permute-start.20) | collective-permute-done | bytes 423968 | tf_op jit(solution)/shard_map/ppermute | solution.py:80
  376.8 7.9 %collective-permute-done.27 = bf16[184,1152]{1,0:T(8,128)(2,1)S(1)} collective-permute-done((bf16[184,1152]{1,0:T(8,128)(2,1)S(1)}, bf16[184,1152]{1,0:T(8,128)(2,1)S(1)}, u32[]{:S(2)}, u32[]{:S(2)}) %collective-permute-start.27) | collective-permute-done | bytes 423968 | tf_op jit(solution)/shard_map/ppermute | solution.py:80
  400.2 6.6 %collective-permute-done.31 = f32[8564]{0:T(1024)S(1)} collective-permute-done((f32[8564]{0:T(1024)S(1)}, f32[8564]{0:T(1024)S(1)}, u32[]{:S(2)}, u32[]{:S(2)}) %collective-permute-start.31) | collective-permute-done | bytes 34288 | tf_op jit(solution)/shard_map/ppermute | solution.py:83
  408.2 5.8 %collective-permute-done.32 = f32[8564]{0:T(1024)S(1)} collective-permute-done((f32[8564]{0:T(1024)S(1)}, f32[8564]{0:T(1024)S(1)}, u32[]{:S(2)}, u32[]{:S(2)}) %collective-permute-start.32) | collective-permute-done | bytes 34288 | tf_op jit(solution)/shard_map/ppermute | solution.py:83
  420.8 66.9 %reduce-scatter.9.cloned.1.call-done = bf16[144,2304]{1,0:T(8,128)(2,1)} async-done(((bf16[1152,2304]{1,0:T(8,128)(2,1)}), bf16[144,2304]{1,0:T(8,128)(2,1)}) %reduce-scatter.9.cloned.1.call-update) | async-done | bytes 663568
  (595 shorter events, 212.1 us)
Async XLA Ops:
  7.2 67.7 %all-gather.4.cloned.1.call-start = ((), (), s32[]{:S(2)}) async-start(), calls=%async_computation.2 | async-start | bytes 2985984 | tf_op jit(solution)/shard_map/all_gather | solution.py:121
  9.3 165.5 %all-gather.6.cloned.1.call-start = ((), (), s32[]{:S(2)}) async-start(), calls=%async_computation.3 | async-start | bytes 5971968 | tf_op jit(solution)/shard_map/all_gather | solution.py:128
  11.6 44.8 %collective-permute-start = (bf16[184,1152]{1,0:T(8,128)(2,1)S(1)}, bf16[184,1152]{1,0:T(8,128)(2,1)S(1)}, u32[]{:S(2)}, u32[]{:S(2)}) collective-permute-start(bf16[184,1152]{1,0:T(8,128)(2,1)S(1)} %get-tuple-element.187), channel_id=1, source_target_pairs={{0,2},{1,3},{2,0},{3,1},{4,6},{5,7},{6,4},{7,5},{8,10},{9,11},{10,... | collective-permute-start | bytes 1271816 | tf_op jit(solution)/shard_map/ppermute | solution.py:80
  14.6 40.3 %collective-permute-start.7 = (bf16[184,1152]{1,0:T(8,128)(2,1)S(1)}, bf16[184,1152]{1,0:T(8,128)(2,1)S(1)}, u32[]{:S(2)}, u32[]{:S(2)}) collective-permute-start(bf16[184,1152]{1,0:T(8,128)(2,1)S(1)} %get-tuple-element.188), channel_id=1, source_target_pairs={{0,2},{1,3},{2,0},{3,1},{4,6},{5,7},{6,4},{7,5},{8,10},{9,11},{10,... | collective-permute-start | bytes 1271816 | tf_op jit(solution)/shard_map/ppermute | solution.py:80
  15.8 42.7 %collective-permute-start.14 = (bf16[184,1152]{1,0:T(8,128)(2,1)S(1)}, bf16[184,1152]{1,0:T(8,128)(2,1)S(1)}, u32[]{:S(2)}, u32[]{:S(2)}) collective-permute-start(bf16[184,1152]{1,0:T(8,128)(2,1)S(1)} %get-tuple-element.171), channel_id=1, source_target_pairs={{0,2},{1,3},{2,0},{3,1},{4,6},{5,7},{6,4},{7,5},{8,10},{9,11},{10,... | collective-permute-start | bytes 1271816 | tf_op jit(solution)/shard_map/ppermute | solution.py:80
  17.7 40.5 %collective-permute-start.21 = (bf16[184,1152]{1,0:T(8,128)(2,1)S(1)}, bf16[184,1152]{1,0:T(8,128)(2,1)S(1)}, u32[]{:S(2)}, u32[]{:S(2)}) collective-permute-start(bf16[184,1152]{1,0:T(8,128)(2,1)S(1)} %get-tuple-element.172), channel_id=1, source_target_pairs={{0,2},{1,3},{2,0},{3,1},{4,6},{5,7},{6,4},{7,5},{8,10},{9,11},{10,... | collective-permute-start | bytes 1271816 | tf_op jit(solution)/shard_map/ppermute | solution.py:80
  19.8 396.2 %reduce-scatter.7.cloned.1.call-start = ((), (), s32[]{:S(2)}) async-start(), calls=%async_computation.4 | async-start | bytes 2985984
  58.5 7.0 %collective-permute-start.15 = (bf16[2,184,1152]{2,1,0:T(8,128)(2,1)S(1)}, bf16[2,184,1152]{2,1,0:T(8,128)(2,1)S(1)}, u32[]{:S(2)}, u32[]{:S(2)}) collective-permute-start(bf16[2,184,1152]{2,1,0:T(8,128)(2,1)S(1)} %pad_maximum_fusion.18), channel_id=1, source_target_pairs={{0,1},{1,0},{2,3},{3,2},{4,5},{5,4},{6,7},{7,6},{8,9},{9,8},{10,11... | collective-permute-start | bytes 2543624 | tf_op jit(solution)/shard_map/ppermute | solution.py:80
  114.7 13.5 %collective-permute-start.9 = (bf16[368,1152]{1,0:T(8,128)(2,1)S(1)}, bf16[368,1152]{1,0:T(8,128)(2,1)S(1)}, u32[]{:S(2)}, u32[]{:S(2)}) collective-permute-start(bf16[368,1152]{1,0:T(8,128)(2,1)S(1)} %pad_maximum_fusion.14), channel_id=1, source_target_pairs={{0,1},{1,0},{2,3},{3,2},{4,5},{5,4},{6,7},{7,6},{8,9},{9,8},{10,11... | collective-permute-start | bytes 2543624 | tf_op jit(solution)/shard_map/ppermute | solution.py:80
  128.5 21.8 %collective-permute-start.10 = (bf16[368,1152]{1,0:T(8,128)(2,1)S(1)}, bf16[368,1152]{1,0:T(8,128)(2,1)S(1)}, u32[]{:S(2)}, u32[]{:S(2)}) collective-permute-start(bf16[368,1152]{1,0:T(8,128)(2,1)S(1)} %pad_maximum_fusion.15), channel_id=1, source_target_pairs={{0,2},{1,3},{2,0},{3,1},{4,6},{5,7},{6,4},{7,5},{8,10},{9,11},{10,... | collective-permute-start | bytes 2543624 | tf_op jit(solution)/shard_map/ppermute | solution.py:80
  130.4 37.2 %collective-permute-start.3 = (bf16[368,1152]{1,0:T(8,128)(2,1)S(1)}, bf16[368,1152]{1,0:T(8,128)(2,1)S(1)}, u32[]{:S(2)}, u32[]{:S(2)}) collective-permute-start(bf16[368,1152]{1,0:T(8,128)(2,1)S(1)} %pad_maximum_fusion.11), channel_id=1, source_target_pairs={{0,2},{1,3},{2,0},{3,1},{4,6},{5,7},{6,4},{7,5},{8,10},{9,11},{10,... | collective-permute-start | bytes 2543624 | tf_op jit(solution)/shard_map/ppermute | solution.py:80
  201.5 21.8 %collective-permute-start.24 = (bf16[368,1152]{1,0:T(8,128)(2,1)S(1)}, bf16[368,1152]{1,0:T(8,128)(2,1)S(1)}, u32[]{:S(2)}, u32[]{:S(2)}) collective-permute-start(bf16[368,1152]{1,0:T(8,128)(2,1)S(1)} %pad_maximum_fusion.24), channel_id=1, source_target_pairs={{0,2},{1,3},{2,0},{3,1},{4,6},{5,7},{6,4},{7,5},{8,10},{9,11},{10,... | collective-permute-start | bytes 2543624 | tf_op jit(solution)/shard_map/ppermute | solution.py:80
  203.3 37.3 %collective-permute-start.17 = (bf16[368,1152]{1,0:T(8,128)(2,1)S(1)}, bf16[368,1152]{1,0:T(8,128)(2,1)S(1)}, u32[]{:S(2)}, u32[]{:S(2)}) collective-permute-start(bf16[368,1152]{1,0:T(8,128)(2,1)S(1)} %pad_maximum_fusion.20), channel_id=1, source_target_pairs={{0,2},{1,3},{2,0},{3,1},{4,6},{5,7},{6,4},{7,5},{8,10},{9,11},{10,... | collective-permute-start | bytes 2543624 | tf_op jit(solution)/shard_map/ppermute | solution.py:80
  210.1 132.8 %collective-permute-start.12 = (bf16[368,1152]{1,0:T(8,128)(2,1)}, bf16[368,1152]{1,0:T(8,128)(2,1)}, u32[]{:S(2)}, u32[]{:S(2)}) collective-permute-start(bf16[368,1152]{1,0:T(8,128)(2,1)} %pad_maximum_fusion.16), channel_id=1, source_target_pairs={{0,1},{1,0},{2,3},{3,2},{4,5},{5,4},{6,7},{7,6},{8,9},{9,8},{10,11... | collective-permute-start | bytes 2543624 | tf_op jit(solution)/shard_map/ppermute | solution.py:80
  246.9 22.3 %collective-permute-start.18 = (bf16[368,1152]{1,0:T(8,128)(2,1)S(1)}, bf16[368,1152]{1,0:T(8,128)(2,1)}, u32[]{:S(2)}, u32[]{:S(2)}) collective-permute-start(bf16[368,1152]{1,0:T(8,128)(2,1)S(1)} %get-tuple-element.92), channel_id=1, source_target_pairs={{0,1},{1,0},{2,3},{3,2},{4,5},{5,4},{6,7},{7,6},{8,9},{9,8},{10,11... | collective-permute-start | bytes 2543624 | tf_op jit(solution)/shard_map/ppermute | solution.py:80
  306.8 180.9 %reduce-scatter.9.cloned.1.call-start = ((), (), s32[]{:S(2)}) async-start(), calls=%async_computation.5 | async-start | bytes 5971968
  340.1 6.5 %collective-permute-start.5 = (bf16[368,1152]{1,0:T(8,128)(2,1)}, bf16[368,1152]{1,0:T(8,128)(2,1)}, u32[]{:S(2)}, u32[]{:S(2)}) collective-permute-start(bf16[368,1152]{1,0:T(8,128)(2,1)} %pad_maximum_fusion.12), channel_id=1, source_target_pairs={{0,1},{1,0},{2,3},{3,2},{4,5},{5,4},{6,7},{7,6},{8,9},{9,8},{10,11... | collective-permute-start | bytes 2543624 | tf_op jit(solution)/shard_map/ppermute | solution.py:80
  345.2 51.4 %collective-permute-start.13 = (bf16[184,1152]{1,0:T(8,128)(2,1)}, bf16[184,1152]{1,0:T(8,128)(2,1)}, u32[]{:S(2)}, u32[]{:S(2)}) collective-permute-start(bf16[184,1152]{1,0:T(8,128)(2,1)} %slice.809), channel_id=1, source_target_pairs={{0,2},{1,3},{2,0},{3,1},{4,6},{5,7},{6,4},{7,5},{8,10},{9,11},{10,... | collective-permute-start | bytes 1271816 | tf_op jit(solution)/shard_map/ppermute | solution.py:80
  348.9 47.8 %collective-permute-start.6 = (bf16[184,1152]{1,0:T(8,128)(2,1)}, bf16[184,1152]{1,0:T(8,128)(2,1)}, u32[]{:S(2)}, u32[]{:S(2)}) collective-permute-start(bf16[184,1152]{1,0:T(8,128)(2,1)} %slice.810), channel_id=1, source_target_pairs={{0,2},{1,3},{2,0},{3,1},{4,6},{5,7},{6,4},{7,5},{8,10},{9,11},{10,... | collective-permute-start | bytes 1271816 | tf_op jit(solution)/shard_map/ppermute | solution.py:80
  353.5 6.9 %collective-permute-start.26 = (bf16[368,1152]{1,0:T(8,128)(2,1)S(1)}, bf16[368,1152]{1,0:T(8,128)(2,1)S(1)}, u32[]{:S(2)}, u32[]{:S(2)}) collective-permute-start(bf16[368,1152]{1,0:T(8,128)(2,1)S(1)} %pad_maximum_fusion.25), channel_id=1, source_target_pairs={{0,1},{1,0},{2,3},{3,2},{4,5},{5,4},{6,7},{7,6},{8,9},{9,8},{10,11... | collective-permute-start | bytes 2543624 | tf_op jit(solution)/shard_map/ppermute | solution.py:80
  359.7 16.6 %collective-permute-start.20 = (bf16[184,1152]{1,0:T(8,128)(2,1)S(1)}, bf16[184,1152]{1,0:T(8,128)(2,1)S(1)}, u32[]{:S(2)}, u32[]{:S(2)}) collective-permute-start(bf16[184,1152]{1,0:T(8,128)(2,1)S(1)} %slice.808), channel_id=1, source_target_pairs={{0,2},{1,3},{2,0},{3,1},{4,6},{5,7},{6,4},{7,5},{8,10},{9,11},{10,... | collective-permute-start | bytes 1271816 | tf_op jit(solution)/shard_map/ppermute | solution.py:80
  360.7 24.0 %collective-permute-start.27 = (bf16[184,1152]{1,0:T(8,128)(2,1)S(1)}, bf16[184,1152]{1,0:T(8,128)(2,1)S(1)}, u32[]{:S(2)}, u32[]{:S(2)}) collective-permute-start(bf16[184,1152]{1,0:T(8,128)(2,1)S(1)} %slice.807), channel_id=1, source_target_pairs={{0,2},{1,3},{2,0},{3,1},{4,6},{5,7},{6,4},{7,5},{8,10},{9,11},{10,... | collective-permute-start | bytes 1271816 | tf_op jit(solution)/shard_map/ppermute | solution.py:80
  399.2 7.6 %collective-permute-start.31 = (f32[8564]{0:T(1024)S(1)}, f32[8564]{0:T(1024)S(1)}, u32[]{:S(2)}, u32[]{:S(2)}) collective-permute-start(f32[8564]{0:T(1024)S(1)} %add.406), channel_id=1, source_target_pairs={{0,8},{4,12},{8,0},{12,4},{16,24},{20,28},{24,16},{28,20},{1,9},{5... | collective-permute-start | bytes 102776 | tf_op jit(solution)/shard_map/ppermute | solution.py:83
  406.8 7.2 %collective-permute-start.32 = (f32[8564]{0:T(1024)S(1)}, f32[8564]{0:T(1024)S(1)}, u32[]{:S(2)}, u32[]{:S(2)}) collective-permute-start(f32[8564]{0:T(1024)S(1)} %add.407), channel_id=1, source_target_pairs={{0,16},{4,20},{8,24},{12,28},{16,0},{20,4},{24,8},{28,12},{1,17},{... | collective-permute-start | bytes 102776 | tf_op jit(solution)/shard_map/ppermute | solution.py:83
  (158 other events, 1188.8 us)
Sparse Core Ops, SparseCore 0:
  10.2 57.9 all-gather.3
  71.0 85.6 all-gather.5
  306.9 72.0 reduce-scatter.6
  382.9 104.7 reduce-scatter.8

commit v2 on v1

v2 whole, which is shorter than its diff:
```python
import functools

import jax
import jax.numpy as jnp
from jax import lax
from jax.experimental import pallas as pl
from jax.experimental.pallas import tpu as pltpu
from jax.sharding import PartitionSpec as P

HD = 72
EPS = 1e-06
BF = jnp.bfloat16
F32 = jnp.float32
LOG2E = 1.4426950408889634
CHUNK = 16
VM = pl.BlockSpec(memory_space=pltpu.VMEM)
SM = pl.BlockSpec(memory_space=pltpu.SMEM)
HBM = pl.BlockSpec(memory_space=pl.ANY)


def dg(a, b, ca, cb):
    return lax.dot_general(a, b, (((ca,), (cb,)), ((), ())), preferred_element_type=F32)


def call(body, name, ins, specs, outs, scratch, flops, exps=0, limit=48):
    shapes = [jax.ShapeDtypeStruct(s, d) for s, d in outs]
    moved = sum(a.size * a.dtype.itemsize for a in ins)
    moved += sum(s.size * s.dtype.itemsize for s in shapes)
    return pl.pallas_call(
        body,
        out_shape=shapes,
        in_specs=specs,
        out_specs=[VM] * len(outs),
        scratch_shapes=scratch,
        compiler_params=pltpu.CompilerParams(vmem_limit_bytes=limit << 20),
        name=name,
        cost_estimate=pl.CostEstimate(
            flops=int(flops), bytes_accessed=int(moved), transcendentals=int(exps)
        ),
    )(*ins)


def normal(x):
    average = jnp.mean(x, -1, keepdims=True)
    center = x - average
    variance = jnp.mean(center * center, -1, keepdims=True)
    inverse = lax.rsqrt(variance + EPS)
    return center * inverse, inverse


def normal_back(hat, inverse, scaled):
    first = jnp.mean(scaled, -1, keepdims=True)
    second = jnp.mean(scaled * hat, -1, keepdims=True)
    return inverse * (scaled - first - hat * second)


def positions(sc_ref, rows, shape, dim):
    r = lax.broadcasted_iota(jnp.int32, shape, dim)
    ti = sc_ref[0]
    p0, p2, p1, p3 = ((ti ^ j) * rows for j in (0, 2, 1, 3))
    return jnp.where(
        r < 2 * rows,
        jnp.where(r < rows, r + p0, r + (p2 - rows)),
        jnp.where(r < 3 * rows, r + (p1 - 2 * rows), r + (p3 - 3 * rows)),
    )


def attn_kernel(heads, rows, slot, sc_ref, xo, xf, xno, xnf, vec_ref, shift_ref, w_ref,
                n1_ref, qkv_ref, mixed_ref, lse_ref, keep_ref, send_ref, s_ref, p_ref):
    seq = 4 * rows
    half = 2 * rows
    hw = heads * HD
    c = LOG2E * HD**-0.5
    gain, bias = vec_ref[0:1, :], vec_ref[1:2, :]
    for i, pair in enumerate(((xo, xf), (xno, xnf))):
        parts = [normal(ref[slot].astype(F32))[0] * gain + bias for ref in pair]
        n1 = jnp.concatenate(parts, 0).astype(BF)
        n1_ref[i * half : (i + 1) * half, :] = n1
        qkv_ref[i * half : (i + 1) * half, :] = (dg(n1, w_ref[...], 1, 0) + shift_ref[...]).astype(BF)
    lane = lax.broadcasted_iota(jnp.int32, (seq, 128), 1)
    pos = positions(sc_ref, rows, (seq, 128), 0)
    mask = jnp.where((lane == HD) & (pos >= sc_ref[1]), -1e30, 0.0).astype(BF)
    one = jnp.where(lane == HD, 1.0, 0.0).astype(BF)
    for h in range(heads):
        a = hw + HD * h
        qx = jnp.where(lane < HD, qkv_ref[:, a : a + 128], one)
        kx = jnp.where(lane < HD, qkv_ref[:, hw + a : hw + a + 128], mask)
        v = qkv_ref[:, 2 * hw + a : 2 * hw + a + HD]
        sl = h % 2
        s_ref[sl] = dg(kx, qx, 1, 1)
        m = s_ref[sl, 0:CHUNK, :]
        for r in range(CHUNK, seq, CHUNK):
            m = jnp.maximum(m, s_ref[sl, r : r + CHUNK, :])
        m = jnp.max(m, 0, keepdims=True) * c
        total = jnp.zeros((CHUNK, seq), F32)
        for r in range(0, seq, CHUNK):
            p = jnp.exp2(s_ref[sl, r : r + CHUNK, :] * c - m)
            total = total + p
            p_ref[sl, r : r + CHUNK, :] = p.astype(BF)
        total = jnp.sum(total, 0, keepdims=True)
        lse_ref[h : h + 1, :] = m + jnp.log2(total)
        mixed = dg(v, p_ref[sl], 0, 0) * (1.0 / total)
        mixed_ref[:, HD * h : HD * h + HD] = mixed.T.astype(BF)
    for i, ref in enumerate((keep_ref, send_ref)):
        ref[...] = dg(mixed_ref[i * half : (i + 1) * half, :], w_ref[:, 0:hw], 1, 1).astype(BF)


def attn(s, sc, blocks, vec, shift, w):
    rows, width = blocks[0].shape[1:]
    seq, hw = 4 * rows, w.shape[1] // 4
    heads = hw // HD
    ins = (sc, *blocks, vec, shift, w)
    outs = [((seq, width), BF), ((seq, 4 * hw), BF), ((seq, hw), BF), ((8, seq), F32)]
    outs += [((2 * rows, width), BF)] * 2
    return call(
        functools.partial(attn_kernel, heads, rows, s), "attn_fwd", ins,
        [SM] + [VM] * 7, outs,
        [pltpu.VMEM((2, seq, seq), F32), pltpu.VMEM((2, seq, seq), BF)],
        2 * seq * width * 5 * hw + 16 * seq * seq * 128 * heads, heads * seq * seq,
    )


def attn_back_kernel(heads, rows, sc_ref, ga_ref, gb_ref, w_ref, qkv_ref, lse_ref,
                     gq_ref, keep_ref, send_ref, col_ref, s_ref, g_ref, p_ref, d_ref, gm_ref):
    seq = 4 * rows
    half = 2 * rows
    hw = heads * HD
    scale = HD**-0.5
    c = LOG2E * scale
    for i, ref in enumerate((ga_ref, gb_ref)):
        gm_ref[i * half : (i + 1) * half, :] = dg(ref[...], w_ref[:, 0:hw], 1, 0).astype(BF)
    lane = lax.broadcasted_iota(jnp.int32, (seq, 128), 1)
    pos = positions(sc_ref, rows, (seq, 128), 0)
    mask = jnp.where((lane == HD) & (pos >= sc_ref[1]), -1e30, 0.0).astype(BF)
    one = jnp.where(lane == HD, 1.0, 0.0).astype(BF)
    gq_ref[:, 0:hw] = jnp.zeros((seq, hw), BF)
    for h in range(heads):
        a = hw + HD * h
        qx = jnp.where(lane < HD, qkv_ref[:, a : a + 128], one)
        kx = jnp.where(lane < HD, qkv_ref[:, hw + a : hw + a + 128], mask)
        q = qkv_ref[:, a : a + HD]
        k = qkv_ref[:, hw + a : hw + a + HD]
        v = qkv_ref[:, 2 * hw + a : 2 * hw + a + HD]
        g = gm_ref[:, HD * h : HD * h + HD]
        sl = h % 2
        s_ref[sl] = dg(kx, qx, 1, 1)
        g_ref[sl] = dg(v, g, 1, 1)
        lse = lse_ref[h : h + 1, :]
        inner = jnp.zeros((CHUNK, seq), F32)
        for r in range(0, seq, CHUNK):
            p = jnp.exp2(s_ref[sl, r : r + CHUNK, :] * c - lse)
            s_ref[sl, r : r + CHUNK, :] = p
            p_ref[sl, r : r + CHUNK, :] = p.astype(BF)
            inner = inner + p * g_ref[sl, r : r + CHUNK, :]
        inner = jnp.sum(inner, 0, keepdims=True)
        for r in range(0, seq, CHUNK):
            d_ref[sl, r : r + CHUNK, :] = (
                s_ref[sl, r : r + CHUNK, :] * (g_ref[sl, r : r + CHUNK, :] - inner)
            ).astype(BF)
        gq_ref[:, a : a + HD] = (dg(k, d_ref[sl], 0, 0) * scale).T.astype(BF)
        gq_ref[:, hw + a : hw + a + HD] = (dg(d_ref[sl], q, 1, 0) * scale).astype(BF)
        gq_ref[:, 2 * hw + a : 2 * hw + a + HD] = dg(p_ref[sl], g, 1, 0).astype(BF)
    col = None
    for i, ref in enumerate((keep_ref, send_ref)):
        part = gq_ref[i * half : (i + 1) * half, :]
        ref[...] = dg(part, w_ref[...], 1, 1).astype(BF)
        now = jnp.sum(part.astype(F32), 0, keepdims=True)
        col = now if col is None else col + now
    col_ref[...] = col


def attn_back(sc, gml, w, qkv, lse):
    half, width = gml[0].shape
    seq, hw = 2 * half, w.shape[1] // 4
    heads = hw // HD
    ins = (sc, *gml, w, qkv, lse)
    outs = [((seq, 4 * hw), BF), ((half, width), BF), ((half, width), BF), ((1, 4 * hw), F32)]
    return call(
        functools.partial(attn_back_kernel, heads, half // 2), "attn_bwd", ins,
        [SM] + [VM] * 5, outs,
        [pltpu.VMEM((2, seq, seq), F32)] * 2 + [pltpu.VMEM((2, seq, seq), BF)] * 2
        + [pltpu.VMEM((seq, hw), BF)],
        2 * seq * width * 5 * hw + 24 * seq * seq * 128 * heads, heads * seq * seq,
    )


def mlp_kernel(rows, slot, sc_ref, na_ref, nb_ref, co, cf, cno, cnf, w_ref, ub_ref,
               act_ref, gh_ref, go_ref, okeep_ref, osend_ref, gkeep_ref, gsend_ref, us_ref):
    half = 2 * rows
    c0 = 0.7978845608028654
    limit = sc_ref[1]
    us = None
    units = ub_ref.shape[1]
    span = w_ref.shape[1] // 2
    wu_ref, wd_ref = w_ref.at[:, 0:units], w_ref.at[:, span : span + units]
    for i, (n_ref, pair, o_ref, g_ref) in enumerate((
        (na_ref, (co, cf), okeep_ref, gkeep_ref),
        (nb_ref, (cno, cnf), osend_ref, gsend_ref),
    )):
        parts = []
        for j, ref in enumerate(pair):
            start = (sc_ref[0] ^ ((0, 2, 1, 3)[2 * i + j])) * rows
            pos = lax.broadcasted_iota(jnp.int32, ref.shape[1:], 0) + start
            parts.append(jnp.where(pos < limit, ref[slot].astype(F32), 0.0))
        go = jnp.concatenate(parts, 0).astype(BF)
        go_ref[i * half : (i + 1) * half, :] = go
        hidden = dg(n_ref[...], wu_ref[...], 1, 0) + ub_ref[...]
        square = hidden * hidden
        t = jnp.tanh(hidden * (c0 + (c0 * 0.044715) * square))
        act = (0.5 * hidden * (1.0 + t)).astype(BF)
        slope = 0.5 * (1.0 + t) + hidden * (1.0 - t * t) * (0.5 * c0 + (1.5 * c0 * 0.044715) * square)
        act_ref[i * half : (i + 1) * half, :] = act
        o_ref[...] = dg(act, wd_ref[...], 1, 1).astype(BF)
        gh = (dg(go, wd_ref[...], 1, 0) * slope).astype(BF)
        gh_ref[i * half : (i + 1) * half, :] = gh
        g_ref[...] = dg(gh, wu_ref[...], 1, 1).astype(BF)
        now = jnp.sum(gh.astype(F32), 0, keepdims=True)
        us = now if us is None else us + now
    us_ref[...] = us


def mlp(s, sc, n2, blocks, w, ub):
    half, width = n2[0].shape
    rows, seq, units = half // 2, 2 * half, ub.shape[1]
    ins = (sc, *n2, *blocks, w, ub)
    outs = [((seq, units), BF), ((seq, units), BF), ((seq, width), BF)]
    outs += [((half, width), BF)] * 4 + [((1, units), F32)]
    return call(
        functools.partial(mlp_kernel, rows, s), "mlp", ins,
        [SM] + [VM] * 8, outs, [],
        8 * seq * width * units, seq * units,
    )


def pair_kernel(n, plan, pad, *refs):
    ins, out = refs[:n], refs[n]
    depth = out.shape[0]
    step = 384 if depth % 384 == 0 else depth
    for at, pairs in plan:
        for a in range(0, depth, step):
            total = None
            for l, r, first in pairs:
                right = ins[r][first : first + ins[l].shape[0], :]
                now = dg(ins[l][:, a : a + step], right, 0, 0)
                total = now if total is None else total + now
            if pad:
                fill = (-total.shape[1]) % 128
                total = jnp.concatenate([total, jnp.zeros((step, fill), F32)], 1)
            out[a : a + step, at : at + total.shape[1]] = total.astype(BF)


def weight_sums(name, depth, width, plan, pad=False, limit=56):
    ins, table, out, flops = [], {}, [], 0

    def index(x):
        if id(x) not in table:
            table[id(x)] = len(ins)
            ins.append(x)
        return table[id(x)]

    for at, pairs in plan:
        out.append((at, [(index(l), index(r), first) for l, r, first in pairs]))
        flops += sum(2 * l.shape[0] * l.shape[1] * r.shape[1] for l, r, _ in pairs)
    return call(
        functools.partial(pair_kernel, len(ins), out, pad), name, tuple(ins), [VM] * len(ins),
        [((depth, width), BF)], [], flops, limit=limit,
    )[0]


def middle_kernel(rows, slot, xo, xf, chip_ref, far_ref, vec_ref, mid_ref, n2_ref):
    parts = []
    for i, ref in enumerate((xo, xf)):
        a, b = i * rows, (1 - i) * rows
        mid = ref[slot].astype(F32) + (
            chip_ref[a : a + rows, :].astype(F32) + far_ref[b : b + rows, :].astype(F32)
        ) + vec_ref[2:3, :]
        mid_ref[a : a + rows, :] = mid
        parts.append(normal(mid)[0] * vec_ref[3:4, :] + vec_ref[4:5, :])
    n2_ref[...] = jnp.concatenate(parts, 0).astype(BF)


def middle_norm(s, xo, xf, chip, far, vec):
    half, width = chip.shape
    rows = half // 2
    return call(
        functools.partial(middle_kernel, rows, s), "middle_norm", (xo, xf, chip, far, vec),
        [VM] * 5, [((half, width), F32), ((half, width), BF)], [], 20 * half * width,
    )


def middle_back_kernel(rows, slot, sc_ref, co, cf, chip_ref, far_ref, mid_ref, vec_ref, gm_ref, gml_ref, sum_ref):
    parts = []
    for i, ref in enumerate((co, cf)):
        a, b = i * rows, (1 - i) * rows
        pos = lax.broadcasted_iota(jnp.int32, ref.shape[1:], 0) + (sc_ref[0] ^ (2 * i)) * rows
        go = jnp.where(pos < sc_ref[1], ref[slot].astype(F32), 0.0)
        grad = chip_ref[a : a + rows, :].astype(F32) + far_ref[b : b + rows, :].astype(F32)
        hat, inverse = normal(mid_ref[a : a + rows, :])
        gm = go + normal_back(hat, inverse, grad * vec_ref[3:4, :])
        parts.append(gm)
        if i == 0:
            gm_ref[...] = gm
            sum_ref[0:1, :] = jnp.sum(gm, 0, keepdims=True)
            sum_ref[1:2, :] = jnp.sum(hat * grad, 0, keepdims=True)
            sum_ref[2:3, :] = jnp.sum(grad, 0, keepdims=True)
            sum_ref[3:4, :] = jnp.sum(go, 0, keepdims=True)
    gml_ref[...] = jnp.concatenate(parts, 0).astype(BF)


def middle_back(s, sc, co, cf, chip, far, mid, vec):
    half, width = chip.shape
    rows = half // 2
    return call(
        functools.partial(middle_back_kernel, rows, s), "middle_bwd", (sc, co, cf, chip, far, mid, vec),
        [SM] + [VM] * 6,
        [((rows, width), F32), ((half, width), BF), ((4, width), F32)], [], 40 * half * width,
    )


def input_back_kernel(rows, slot, xo, keep_ref, near_ref, far_ref, gm_ref, vec_ref, out_ref, sum_ref):
    grad = (
        keep_ref[0:rows, :].astype(F32) + near_ref[0:rows, :].astype(F32) + far_ref[...].astype(F32)
    )
    hat, inverse = normal(xo[slot].astype(F32))
    out_ref[...] = gm_ref[...] + normal_back(hat, inverse, grad * vec_ref[0:1, :])
    sum_ref[0:1, :] = jnp.sum(hat * grad, 0, keepdims=True)
    sum_ref[1:2, :] = jnp.sum(grad, 0, keepdims=True)


def input_back(s, xo, keep, near, far, gm, vec):
    rows, width = far.shape
    return call(
        functools.partial(input_back_kernel, rows, s), "input_bwd", (xo, keep, near, far, gm, vec),
        [VM] * 6, [((rows, width), F32), ((2, width), F32)], [],
        30 * rows * width,
    )


def pack_attn_kernel(q_ref, k_ref, v_ref, o_ref, v0, v1, v2, v3, v4, v5, out_ref):
    shard, hw = q_ref.shape
    out_ref[0:shard, 0:hw] = o_ref[...].astype(F32).T.astype(BF)
    for i, ref in enumerate((q_ref, k_ref, v_ref)):
        out_ref[0:shard, (i + 1) * hw : (i + 2) * hw] = ref[...]
    lines = [ref[...].astype(F32) for ref in (v0, v1, v2, v3, v4, v5)]
    lines = jnp.concatenate(lines + [jnp.zeros((2, shard), F32)], 0)
    lines = jnp.concatenate([lines, jnp.zeros((8, 4 * hw - shard), F32)], 1)
    out_ref[shard : shard + 8, :] = lines.astype(BF)


def pack_mlp_kernel(u_ref, d_ref, out_ref):
    shard, units = u_ref.shape
    span = out_ref.shape[1] // 2
    fill = jnp.zeros((shard, span - units), F32)
    out_ref[:, 0:span] = jnp.concatenate([u_ref[...].astype(F32), fill], 1).astype(BF)
    out_ref[:, span:] = jnp.concatenate([d_ref[...].astype(F32).T, fill], 1).astype(BF)


def place_kernel(n, cuts, idx_ref, *refs):
    sources, outs, sems = refs[:n], refs[n:-1], refs[-1]
    copies = []
    for i, src in enumerate(sources):
        for o, (a, b) in enumerate(cuts):
            dst = outs[o].at[idx_ref[i]]
            copies.append(pltpu.make_async_copy(src.at[a:b], dst, sems.at[len(copies)]))
    for c in copies:
        c.start()
    for c in copies:
        c.wait()


def place_shards(idx, sources, cuts):
    n = len(sources)
    cols = sources[0].shape[1]
    outs = [((n, b - a, cols), BF) for a, b in cuts]
    return call(
        functools.partial(place_kernel, n, cuts), "place_shards", (idx, *sources), [SM] + [HBM] * n,
        outs, [pltpu.SemaphoreType.DMA((n * len(cuts),))], 0, limit=16,
    )


def after(x, *others):
    return lax.optimization_barrier((x, *others))[0]


def local(
    inputs,
    cotangent,
    lengths,
    ln1_gain,
    ln1_bias,
    q_weight,
    q_bias,
    k_weight,
    v_weight,
    v_bias,
    out_weight,
    out_bias,
    ln2_gain,
    ln2_bias,
    up_weight,
    up_bias,
    down_weight,
    down_bias,
):
    tp = lax.axis_size("tp")
    fs = lax.axis_size("fsdp")
    ti = lax.axis_index("tp")
    fi = lax.axis_index("fsdp")
    slots, rows, width = inputs.shape
    half = 2 * rows
    hw = q_weight.shape[1]
    units = up_weight.shape[1]
    shard = width // fs
    zi, yi = fi // 2, fi % 2

    def swap_tp(x, k):
        return lax.ppermute(x, "tp", [(i, i ^ k) for i in range(tp)])

    def swap_fs(x, k):
        return lax.ppermute(x, "fsdp", [(i, i ^ k) for i in range(fs)])

    def turn(x, k):
        return lax.ppermute(x, "fsdp", [(i, (i + 2 * k) % fs) for i in range(fs)])

    def gather_shards(own, cuts, beside, later):
        if fs != 8:
            whole = lax.all_gather(own, "fsdp", axis=0)
            return tuple(whole[:, a:b] for a, b in cuts), beside(own), later(own), whole
        first = lax.optimization_barrier((turn(own, 1), turn(own, 3), swap_fs(own, 1), beside(own)))
        r1, r3, o0, extra = first
        own, r1, r3, extra = lax.optimization_barrier((own, r1, r3, extra))
        second = (turn(own, 2), swap_fs(r1, 1), swap_fs(r3, 1), later(extra))
        r2, o1, o3, extra2 = lax.optimization_barrier(second)
        o2 = swap_fs(r2, 1)
        order = jnp.stack([(zi + 4 - k) % 4 for k in (0, 1, 3, 2)]) * 2
        idx = jnp.concatenate([order + yi, order + 1 - yi]).astype(jnp.int32)
        sources = [own, r1, r3, r2, o0, o1, o3, o2]
        return place_shards(idx, sources, cuts), extra, extra2, r1

    def scatter_sums(total):
        if fs != 8:
            return lax.psum_scatter(total, "fsdp", scatter_dimension=0, tiled=True).astype(F32)
        cols = total.shape[1]
        parts = total.reshape(4, 2, shard, cols)

        def pick(k, y):
            return lax.dynamic_slice(parts, ((zi + k) % 4, y, 0, 0), (1, 1, shard, cols))[0, 0]

        first = swap_fs(jnp.stack([pick(k, 1 - yi) for k in (1, 3, 2)], 0), 1)
        mine = swap_fs(pick(0, 1 - yi), 1)
        got = []
        for j, k in enumerate((1, 3, 2)):
            got.append(turn((pick(k, yi).astype(F32) + first[j].astype(F32)).astype(BF), k))
        mine = pick(0, yi).astype(F32) + mine.astype(F32)
        return mine + (got[0].astype(F32) + got[1].astype(F32)) + got[2].astype(F32)

    def chip_sum(keep, send):
        return (keep.astype(F32) + swap_tp(send, 1).astype(F32)).astype(BF)

    def own_part(keep, send):
        near = swap_tp(send, 1)
        far = (keep[rows:].astype(F32) + near[rows:].astype(F32)).astype(BF)
        return near, swap_tp(far, 2)

    lines = [a[None, :] for a in (ln1_gain, ln1_bias, out_bias, ln2_gain, ln2_bias, down_bias)]
    pack = call(
        pack_attn_kernel, "pack_attn", (q_weight, k_weight, v_weight, out_weight, *lines), [VM] * 10,
        [((shard + 8, 4 * hw), BF)], [], 0,
    )[0]
    (w_attn, small), x_far, c_far, sent = gather_shards(
        pack,
        ((0, shard), (shard, shard + 8)),
        lambda _: swap_tp(inputs, 2),
        lambda x: swap_tp(after(cotangent, x), 2),
    )
    x_blocks = (inputs, x_far, swap_tp(inputs, 1), swap_tp(x_far, 1))
    c_blocks = (cotangent, c_far, swap_tp(cotangent, 1), swap_tp(c_far, 1))
    w_attn = w_attn.reshape(width, 4 * hw)
    vec = small[:, :, :shard].transpose(1, 0, 2).reshape(8, width).astype(F32)
    span = units + (-units) % 128
    pack = call(
        pack_mlp_kernel, "pack_mlp", (up_weight, down_weight), [VM] * 2, [((shard, 2 * span), BF)], [], 0
    )[0]
    w_mlp = lax.all_gather(after(pack, sent), "fsdp", axis=0, tiled=True)

    none = jnp.zeros_like(q_bias)
    shift = jnp.concatenate([none, q_bias, none, v_bias], 0).astype(F32)[None, :]
    ub = up_bias.astype(F32)[None, :]
    scalars = [jnp.stack([ti, lengths[s]]).astype(jnp.int32) for s in range(slots)]

    every = range(slots)
    fwd, chips, mids, mlps = [], [], [], []
    w_now = w_attn
    for s in every:
        fwd.append(attn(s, scalars[s], x_blocks, vec, shift, w_now))
        chip = chip_sum(fwd[s][4], fwd[s][5])
        if s < slots - 1:
            chip, w_now = lax.optimization_barrier((chip, w_now))
        chips.append(chip)
    for s in every:
        mid, n2 = middle_norm(s, x_blocks[0], x_blocks[1], chips[s], swap_tp(chips[s], 2), vec)
        mids.append((mid, (n2, swap_tp(n2, 1))))
    chips = []
    w_now = w_mlp
    for s in every:
        mlps.append(mlp(s, scalars[s], mids[s][1], c_blocks, w_now, ub))
        chip = chip_sum(mlps[s][5], mlps[s][6])
        if s < slots - 1:
            chip, w_now = lax.optimization_barrier((chip, w_now))
        chips.append(chip)
    fars = [swap_tp(c, 2) for c in chips]
    ups, downs = [], []
    for s in every:
        act, gh, go = mlps[s][:3]
        if s == 0:
            act, fars[0] = lax.optimization_barrier((act, fars[0]))
        downs.append((go, act, 0))
        ups += [(mids[s][1][i], gh, i * half) for i in range(2)]
    g_mlp = weight_sums("mlp_dw", width, 2 * span, [(0, ups), (span, downs)], units % 128 > 0)
    r_mlp = lax.psum_scatter(g_mlp, "fsdp", scatter_dimension=0, tiled=True).astype(F32)
    outs, grads_x = [], []
    wide = cols = None
    heads_out, heads_in = [], []
    mid_now = [m[0] for m in mids]
    for s in every:
        okeep, osend = mlps[s][3:5]
        gm, gml, sums = middle_back(
            s, scalars[s], c_blocks[0], c_blocks[1], chips[s], fars[s], mid_now[s], vec
        )
        gml = (gml, swap_tp(gml, 1))
        n1, qkv, mixed, lse = fwd[s][:4]
        gqkv, keep, send, col = attn_back(scalars[s], gml, w_attn, qkv, lse)
        if s < slots - 1:
            mid_now[s + 1], col = lax.optimization_barrier((mid_now[s + 1], col))
        near, far = own_part(keep, send)
        grad, sums1 = input_back(s, x_blocks[0], keep, near, far, gm, vec)
        grads_x.append(grad)
        near, far = own_part(okeep, osend)
        outs.append(
            (
                mids[s][0][:rows]
                + (okeep[:rows].astype(F32) + near[:rows].astype(F32) + far.astype(F32))
                + vec[5:6]
            ).astype(BF)
        )
        now = jnp.concatenate([sums1, sums], 0)
        wide = now if wide is None else wide + now
        cols = col if cols is None else cols + col
        heads_out += [(gml[i], mixed, i * half) for i in range(2)]
        heads_in.append((n1, gqkv, 0))
    g_attn = weight_sums("attn_dw", width, 4 * hw, [(0, heads_in), (0, heads_out)])
    r_attn = scatter_sums(g_attn)

    unit_sums = sum(m[7] for m in mlps)
    wide = wide + swap_tp(wide, 1)
    wide = wide + swap_tp(wide, 2)
    flat = jnp.concatenate(
        [wide.reshape(-1), cols[0, hw : 2 * hw], cols[0, 3 * hw :], unit_sums[0]], 0
    )
    step = 1
    while step < fs:
        flat = flat + swap_fs(flat, step)
        step *= 2
    wide = flat[: 6 * width].reshape(6, width)
    wide = lax.dynamic_slice_in_dim(wide, fi * shard, shard, 1)
    tail = flat[6 * width :]
    return (
        jnp.stack(outs, 0),
        jnp.stack(grads_x, 0),
        wide[0],
        wide[1],
        r_attn[:, hw : 2 * hw],
        tail[:hw],
        r_attn[:, 2 * hw : 3 * hw],
        r_attn[:, 3 * hw :],
        tail[hw : 2 * hw],
        r_attn[:, :hw].T,
        wide[2],
        wide[3],
        wide[4],
        r_mlp[:, :units],
        tail[2 * hw :],
        r_mlp[:, span : span + units].T,
        wide[5],
    )


def solution(mesh):
    rowed = P("fsdp", "tp", None)
    wide = P("fsdp")
    cols = P("fsdp", "tp")
    turned = P("tp", "fsdp")
    part = P("tp")
    in_specs = (
        rowed, rowed, wide, wide, wide, cols, part, cols, cols, part, turned, wide,
        wide, wide, cols, part, turned, wide,
    )
    out_specs = (
        rowed, rowed, wide, wide, cols, part, cols, cols, part, turned, wide, wide, wide,
        cols, part, turned, wide,
    )
    return jax.shard_map(local, mesh=mesh, in_specs=in_specs, out_specs=out_specs, check_vma=False)
```

time: 508 us -> 354 us (0.70)
  Pallas kernels: 0 us -> 128 us
  matrix products: 108 us -> 0 us
  waiting for transfers between devices: 175 us -> 110 us
  other arithmetic: 67.2 us -> 14.5 us
  local copies, waits for them, and re-layouts: 79.9 us -> 42.8 us
  blocking collectives: 31.5 us -> 0 us
  starting transfers between devices: 22.3 us -> 40.8 us
    pallas_call x0 -> x17, Pallas kernels: none -> 128 us  [call(): pl.pallas_call(body, out_shape=shapes, in_specs=specs, out_specs=[VM] * l...]
    dot_general x36 -> x0, matrix products: 108 us -> none  [the longest x8 34 us: dot_nn(): lax.dot_general(a, b, (((1,), (0,)), ((), ())), preferred_element_type=F32)]
    ppermute x30 -> x28, waiting for transfers between devices: 95 us -> 25.4 us  [swap_tp(): return lax.ppermute(x, 'tp', [(i, i ^ k) for i in range(tp)])]
    unnamed x6 -> x2, waiting for transfers between devices: 67 us -> 0.03 us
    ppermute x0 -> x6, waiting for transfers between devices: none -> 54.6 us  [turn(): return lax.ppermute(x, 'fsdp', [(i, (i + 2 * k) % fs) for i in range(fs)])]
    all_gather x1 -> x0, blocking collectives: 31.5 us -> none  [local(): small = lax.all_gather(small, 'fsdp', axis=0)]
    slice x52 -> x6, local copies, waits for them, and re-layouts: 33.2 us -> 2.87 us  [the longest x1 0.87 us: local(): vec[5:6]]
    reduce_sum x22 -> x0, other arithmetic: 17 us -> none  [the longest x2 4.54 us: local(): lse = top + jnp.log(jnp.sum(jnp.exp(scores - top), -1, keepdims=True))]
  transfers between devices with their start and end apart: 37 -> 45, of which waited for: 15 -> 16; matrix products, arithmetic and copies ran while one was open for 42% -> 8% of each run, Pallas kernels for 0% -> 31%
where the time goes in v2:
time: 354 us; the launch traced here: 350 us
  Pallas kernels  128 us (36%)
  waiting for transfers between devices  110 us (31%)
  local copies, waits for them, and re-layouts  42.8 us (12%)
  starting transfers between devices  40.8 us (12%)
  between operations  14.8 us (4%)
  other arithmetic  14.5 us (4%)
    pallas_call x17, Pallas kernels, call(): pl.pallas_call(body, out_shape=shapes, in_specs=specs, out_specs=[VM] * l...  128 us
    ppermute x6, waiting for transfers between devices, turn(): return lax.ppermute(x, 'fsdp', [(i, (i + 2 * k) % fs) for i in range(fs)])  54.6 us
    unnamed x114, local copies, waits for them, and re-layouts  29.8 us
    ppermute x9, waiting for transfers between devices, swap_fs(): return lax.ppermute(x, 'fsdp', [(i, i ^ k) for i in range(fs)])  29.7 us
    ppermute x28, waiting for transfers between devices, swap_tp(): return lax.ppermute(x, 'tp', [(i, i ^ k) for i in range(tp)])  25.4 us
    ppermute x9, starting transfers between devices, swap_fs(): return lax.ppermute(x, 'fsdp', [(i, i ^ k) for i in range(fs)])  17.3 us
    ppermute x28, starting transfers between devices, swap_tp(): return lax.ppermute(x, 'tp', [(i, i ^ k) for i in range(tp)])  15.7 us
    ppermute x6, starting transfers between devices, turn(): return lax.ppermute(x, 'fsdp', [(i, (i + 2 * k) % fs) for i in range(fs)])  7.73 us
  transfers between devices with their start and end apart: 45, of which 16 were waited for; matrix products, arithmetic and copies ran while one was open for 8% of the time, Pallas kernels for 31%

profile of v2, /device:TPU:0, one launch (start us, length us, event | category | flops | bytes accessed | tf_op | source)
XLA Modules:
  0.0 350.4 jit_solution(14171392247754892960)
XLA Ops:
  7.2 3.0 collective-permute-start.3
  27.5 4.6 %collective-permute-done.refs_1_ = bf16[152,1152]{1,0:T(8,128)(2,1)S(1)} collective-permute-done((bf16[152,1152]{1,0:T(8,128)(2,1)}, bf16[152,1152]{1,0:T(8,128)(2,1)S(1)}, u32[]{:S(2)}, u32[]{:S(2)}) %collective-permute-start) | collective-permute-done | bytes 350240 | tf_op jit(solution)/shard_map/ppermute | solution.py:423
  32.1 5.6 %collective-permute-done.1.refs_2_ = bf16[152,1152]{1,0:T(8,128)(2,1)} collective-permute-done((bf16[152,1152]{1,0:T(8,128)(2,1)}, bf16[152,1152]{1,0:T(8,128)(2,1)}, u32[]{:S(2)}, u32[]{:S(2)}) %collective-permute-start.1) | collective-permute-done | bytes 350240 | tf_op jit(solution)/shard_map/ppermute | solution.py:423
  42.2 32.4 %collective-permute-done.6.refs_3_ = bf16[152,1152]{1,0:T(8,128)(2,1)} collective-permute-done((bf16[152,1152]{1,0:T(8,128)(2,1)}, bf16[152,1152]{1,0:T(8,128)(2,1)}, u32[]{:S(2)}, u32[]{:S(2)}) %collective-permute-start.6) | collective-permute-done | bytes 350240 | tf_op jit(solution)/shard_map/ppermute | solution.py:423
  77.8 10.4 %collective-permute-done.10.refs_7_ = bf16[152,1152]{1,0:T(8,128)(2,1)} collective-permute-done((bf16[152,1152]{1,0:T(8,128)(2,1)}, bf16[152,1152]{1,0:T(8,128)(2,1)}, u32[]{:S(2)}, u32[]{:S(2)}) %collective-permute-start.10) | collective-permute-done | bytes 350240 | tf_op jit(solution)/shard_map/ppermute | solution.py:420
  89.2 2.6 place_shards.1
  94.1 10.8 %attn_fwd.2 = (bf16[736,1152]{1,0:T(8,128)(2,1)}, bf16[736,1152]{1,0:T(8,128)(2,1)}, bf16[736,288]{1,0:T(8,128)(2,1)S(1)}, f32[8,736]{1,0:T(8,128)S(1)}, bf16[36...) custom-call(s32[2]{0:T(128)S(1)} %pad_add_fusion.sc_ref, bf16[2,184,1152]{2,1,0:T(8,128)(2,1)S(1)} %copy-done, ...), custom_call_target="tpu_custom_call" | custom-call | flops 6879444992 | bytes 11621896 | tf_op jit(solution)/shard_map/attn_fwd/pallas_call | solution.py:29
  108.9 11.0 %attn_fwd.3 = (bf16[736,1152]{1,0:T(8,128)(2,1)}, bf16[736,1152]{1,0:T(8,128)(2,1)}, bf16[736,288]{1,0:T(8,128)(2,1)S(1)}, f32[8,736]{1,0:T(8,128)S(1)}, bf16[36...) custom-call(s32[2]{0:T(128)S(1)} %pad_add_fusion.2.sc_ref, bf16[2,184,1152]{2,1,0:T(8,128)(2,1)S(1)} %copy-done, ...), custom_call_target="tpu_custom_call" | custom-call | flops 6879444992 | bytes 11621896 | tf_op jit(solution)/shard_map/attn_fwd/pallas_call | solution.py:29
  121.2 7.2 %collective-permute-done.12.far_ref = bf16[368,1152]{1,0:T(8,128)(2,1)S(1)} collective-permute-done((bf16[368,1152]{1,0:T(8,128)(2,1)S(1)}, bf16[368,1152]{1,0:T(8,128)(2,1)S(1)}, u32[]{:S(2)}, u32[]{:S(2)}) %collective-permute-start.12) | collective-permute-done | bytes 847904 | tf_op jit(solution)/shard_map/ppermute | solution.py:417
  137.3 14.8 %mlp.2 = (bf16[736,1076]{1,0:T(8,128)(2,1)}, bf16[736,1076]{1,0:T(8,128)(2,1)}, bf16[736,1152]{1,0:T(8,128)(2,1)}, bf16[368,1152]{1,0:T(8,128)(2,1)S(1)}, bf16[3...) custom-call(s32[2]{0:T(128)S(1)} %pad_add_fusion.sc_ref, ...), custom_call_target="tpu_custom_call" | custom-call | flops 7298482176 | bytes 18659240 | tf_op jit(solution)/shard_map/mlp/pallas_call | solution.py:29
  160.8 14.8 %mlp.3 = (bf16[736,1076]{1,0:T(8,128)(2,1)}, bf16[736,1076]{1,0:T(8,128)(2,1)}, bf16[736,1152]{1,0:T(8,128)(2,1)}, bf16[368,1152]{1,0:T(8,128)(2,1)S(1)}, bf16[3...) custom-call(s32[2]{0:T(128)S(1)} %pad_add_fusion.2.sc_ref, ...), custom_call_target="tpu_custom_call" | custom-call | flops 7298482176 | bytes 18659240 | tf_op jit(solution)/shard_map/mlp/pallas_call | solution.py:29
  180.9 17.9 %mlp_dw.1 = bf16[1152,2304]{1,0:T(8,128)(2,1)} custom-call(bf16[368,1152]{1,0:T(8,128)(2,1)} %copy-done.32, bf16[736,1076]{1,0:T(8,128)(2,1)} %get-tuple-element.159.refs_1_, bf16[368,1152]{1,0:T(8,128)(2,1)} %copy-done.34, bf16[368,1152]{1,0:T(8,128)(2,1)} %copy-done.38, bf16[736,1076]{1,0:T(8,128)(2,1)} %get-tuple-element.160.refs_4_, ...), custom_call_target="tpu_custom_call" | custom-call | flops 7298482176 | bytes 18426880 | tf_op jit(solution)/shard_map/mlp_dw/pallas_call | solution.py:29
  201.2 3.8 %middle_bwd.2 = (f32[184,1152]{1,0:T(8,128)S(1)}, bf16[368,1152]{1,0:T(8,128)(2,1)}, f32[4,1152]{1,0:T(4,128)S(1)}) custom-call(s32[2]{0:T(128)S(1)} %pad_add_fusion.sc_ref, bf16[2,184,1152]{2,1,0:T(8,128)(2,1)S(1)} %copy-done.5, bf16[2,184,1152]{2,1,0:T(8,128)(2,1)S(1)} %copy-done.7, bf16[368,1152]{1,0:T(8,128)(2,1)S(1)} %add_convert_fusion.1.chip_ref, ...), custom_call_target="tpu_custom_call" | custom-call | flops 16957440 | bytes 6838280 | tf_op jit(solution)/shard_map/middle_bwd/pallas_call | solution.py:29
  209.8 14.2 %attn_bwd.2 = (bf16[736,1152]{1,0:T(8,128)(2,1)S(1)}, bf16[368,1152]{1,0:T(8,128)(2,1)S(1)}, bf16[368,1152]{1,0:T(8,128)(2,1)S(1)}, f32[1,1152]{1,0:T(1,128)S(1)}) custom-call(s32[2]{0:T(128)S(1)} %pad_add_fusion.sc_ref, bf16[368,1152]{1,0:T(8,128)(2,1)} %get-tuple-element.127.ga_ref.refs_4_, bf16[368,1152]{1,0:T(8,128)(2,1)S(1)} %collective-permute-done.25.gb_ref.refs_6_, ...), custom_call_target="tpu_custom_call" | custom-call | flops 9098231808 | bytes 9465352 | tf_op jit(solution)/shard_map/attn_bwd/pallas_call | solution.py:29
  225.3 5.1 %collective-permute-done.29.far_ref = bf16[368,1152]{1,0:T(8,128)(2,1)S(1)} collective-permute-done((bf16[368,1152]{1,0:T(8,128)(2,1)S(1)}, bf16[368,1152]{1,0:T(8,128)(2,1)S(1)}, u32[]{:S(2)}, u32[]{:S(2)}) %collective-permute-start.29) | collective-permute-done | bytes 847904 | tf_op jit(solution)/shard_map/ppermute | solution.py:417
  230.4 3.0 middle_bwd.3
  237.7 15.1 %attn_bwd.3 = (bf16[736,1152]{1,0:T(8,128)(2,1)S(1)}, bf16[368,1152]{1,0:T(8,128)(2,1)S(1)}, bf16[368,1152]{1,0:T(8,128)(2,1)}, f32[1,1152]{1,0:T(1,128)S(1)}) custom-call(s32[2]{0:T(128)S(1)} %pad_add_fusion.2.sc_ref, bf16[368,1152]{1,0:T(8,128)(2,1)S(1)} %get-tuple-element.138.ga_ref.refs_7_, bf16[368,1152]{1,0:T(8,128)(2,1)S(1)} %collective-permute-done.30.gb_ref.refs_9_, ...), custom_call_target="tpu_custom_call" | custom-call | flops 9098231808 | bytes 9465352 | tf_op jit(solution)/shard_map/attn_bwd/pallas_call | solution.py:29
  255.5 13.1 %attn_dw.1 = bf16[1152,1152]{1,0:T(8,128)(2,1)} custom-call(bf16[736,1152]{1,0:T(8,128)(2,1)} %get-tuple-element.153.refs_0_, bf16[736,1152]{1,0:T(8,128)(2,1)} %copy-done.40, bf16[736,1152]{1,0:T(8,128)(2,1)} %get-tuple-element.155.refs_2_, bf16[736,1152]{1,0:T(8,128)(2,1)} %copy-done.41, bf16[368,1152]{1,0:T(8,128)(2,1)} %get-tuple-element.127.ga_ref.refs_4_, ...), custom_call_target="tpu_custom_call" | custom-call | flops 4883742720 | bytes 13676544 | tf_op jit(solution)/shard_map/attn_dw/pallas_call | solution.py:29
  271.0 2.5 collective-permute-start.39
  278.8 5.9 %collective-permute-done.32.far_ref = bf16[184,1152]{1,0:T(8,128)(2,1)S(1)} collective-permute-done((bf16[184,1152]{1,0:T(8,128)(2,1)S(1)}, bf16[184,1152]{1,0:T(8,128)(2,1)S(1)}, u32[]{:S(2)}, u32[]{:S(2)}) %collective-permute-start.32) | collective-permute-done | bytes 423968 | tf_op jit(solution)/shard_map/ppermute | solution.py:417
  285.7 17.8 %collective-permute-done.39 = bf16[3,144,1152]{2,1,0:T(8,128)(2,1)S(1)} collective-permute-done((bf16[3,144,1152]{2,1,0:T(8,128)(2,1)S(1)}, bf16[3,144,1152]{2,1,0:T(8,128)(2,1)S(1)}, u32[]{:S(2)}, u32[]{:S(2)}) %collective-permute-start.39) | collective-permute-done | bytes 995360 | tf_op jit(solution)/shard_map/ppermute | solution.py:420
  308.5 2.6 collective-permute-done.34
  316.6 10.3 %collective-permute-done.42 = bf16[144,1152]{1,0:T(8,128)(2,1)S(1)} collective-permute-done((bf16[144,1152]{1,0:T(8,128)(2,1)S(1)}, bf16[144,1152]{1,0:T(8,128)(2,1)S(1)}, u32[]{:S(2)}, u32[]{:S(2)}) %collective-permute-start.42) | collective-permute-done | bytes 331808 | tf_op jit(solution)/shard_map/ppermute | solution.py:423
  330.1 6.3 %collective-permute-start.37 = (f32[8564]{0:T(1024)S(1)}, f32[8564]{0:T(1024)S(1)}, u32[]{:S(2)}, u32[]{:S(2)}) collective-permute-start(f32[8564]{0:T(1024)S(1)} %add.227), channel_id=1, source_target_pairs={{0,16},{4,20},{8,24},{12,28},{16,0},{20,4},{24,8},{28,12},{1,17},{... | collective-permute-start | bytes 102776 | tf_op jit(solution)/shard_map/ppermute | solution.py:420
  (257 shorter events, 100.6 us)
Async XLA Ops:
  7.2 127.8 %all-gather.2.cloned.1.call-start = ((), (), s32[]{:S(2)}) async-start(), calls=%async_computation.1 | async-start | bytes 5971968 | tf_op jit(solution)/shard_map/all_gather | solution.py:484
  7.2 30.4 %collective-permute-start.3 = (bf16[2,184,1152]{2,1,0:T(8,128)(2,1)}, bf16[2,184,1152]{2,1,0:T(8,128)(2,1)S(1)}, u32[]{:S(2)}, u32[]{:S(2)}) collective-permute-start(bf16[2,184,1152]{2,1,0:T(8,128)(2,1)} %xo.11), channel_id=1, source_target_pairs={{0,2},{1,3},{2,0},{3,1},{4,6},{5,7},{6,4},{7,5},{8,10},{9,11},{10,... | collective-permute-start | bytes 2543624 | tf_op jit(solution)/shard_map/ppermute | solution.py:417
  37.7 302.6 %reduce-scatter.2.cloned.1.call-start = ((), (), s32[]{:S(2)}) async-start(), calls=%async_computation.2 | async-start | bytes 5971968 | tf_op jit(solution)/shard_map/reduce_scatter | solution.py:520
  37.8 37.5 %collective-permute-start.9 = (bf16[2,184,1152]{2,1,0:T(8,128)(2,1)S(1)}, bf16[2,184,1152]{2,1,0:T(8,128)(2,1)S(1)}, u32[]{:S(2)}, u32[]{:S(2)}) collective-permute-start(bf16[2,184,1152]{2,1,0:T(8,128)(2,1)S(1)} %copy-done.5), channel_id=1, source_target_pairs={{0,2},{1,3},{2,0},{3,1},{4,6},{5,7},{6,4},{7,5},{8,10},{9,11},{10,... | collective-permute-start | bytes 2543624 | tf_op jit(solution)/shard_map/ppermute | solution.py:417
  38.4 36.2 %collective-permute-start.6 = (bf16[152,1152]{1,0:T(8,128)(2,1)}, bf16[152,1152]{1,0:T(8,128)(2,1)}, u32[]{:S(2)}, u32[]{:S(2)}) collective-permute-start(bf16[152,1152]{1,0:T(8,128)(2,1)} %pack_attn.1.refs_0_), channel_id=1, source_target_pairs={{0,16},{4,20},{8,24},{12,28},{16,0},{20,4},{24,8},{28,12},{1,17},{... | collective-permute-start | bytes 1050632 | tf_op jit(solution)/shard_map/ppermute | solution.py:423
  40.1 35.1 %collective-permute-start.7 = (bf16[152,1152]{1,0:T(8,128)(2,1)}, bf16[152,1152]{1,0:T(8,128)(2,1)}, u32[]{:S(2)}, u32[]{:S(2)}) collective-permute-start(bf16[152,1152]{1,0:T(8,128)(2,1)} %copy-done.21), channel_id=1, source_target_pairs={{0,4},{4,0},{8,12},{12,8},{16,20},{20,16},{24,28},{28,24},{1,5},{5... | collective-permute-start | bytes 1050632 | tf_op jit(solution)/shard_map/ppermute | solution.py:420
  41.6 33.6 %collective-permute-start.8 = (bf16[152,1152]{1,0:T(8,128)(2,1)}, bf16[152,1152]{1,0:T(8,128)(2,1)}, u32[]{:S(2)}, u32[]{:S(2)}) collective-permute-start(bf16[152,1152]{1,0:T(8,128)(2,1)} %collective-permute-done.1.refs_2_), channel_id=1, source_target_pairs={{0,4},{4,0},{8,12},{12,8},{16,20},{20,16},{24,28},{28,24},{1,5},{5... | collective-permute-start | bytes 1050632 | tf_op jit(solution)/shard_map/ppermute | solution.py:420
  42.2 52.0 %collective-permute-start.4 = (bf16[2,184,1152]{2,1,0:T(8,128)(2,1)S(1)}, bf16[2,184,1152]{2,1,0:T(8,128)(2,1)}, u32[]{:S(2)}, u32[]{:S(2)}) collective-permute-start(bf16[2,184,1152]{2,1,0:T(8,128)(2,1)S(1)} %copy-done), channel_id=1, source_target_pairs={{0,1},{1,0},{2,3},{3,2},{4,5},{5,4},{6,7},{7,6},{8,9},{9,8},{10,11... | collective-permute-start | bytes 2543624 | tf_op jit(solution)/shard_map/ppermute | solution.py:417
  74.6 19.5 %collective-permute-start.5 = (bf16[2,184,1152]{2,1,0:T(8,128)(2,1)S(1)}, bf16[2,184,1152]{2,1,0:T(8,128)(2,1)}, u32[]{:S(2)}, u32[]{:S(2)}) collective-permute-start(bf16[2,184,1152]{2,1,0:T(8,128)(2,1)S(1)} %collective-permute-done.3.xf), channel_id=1, source_target_pairs={{0,1},{1,0},{2,3},{3,2},{4,5},{5,4},{6,7},{7,6},{8,9},{9,8},{10,11... | collective-permute-start | bytes 2543624 | tf_op jit(solution)/shard_map/ppermute | solution.py:417
  107.5 21.0 %collective-permute-start.12 = (bf16[368,1152]{1,0:T(8,128)(2,1)S(1)}, bf16[368,1152]{1,0:T(8,128)(2,1)S(1)}, u32[]{:S(2)}, u32[]{:S(2)}) collective-permute-start(bf16[368,1152]{1,0:T(8,128)(2,1)S(1)} %add_convert_fusion.3.chip_ref), channel_id=1, source_target_pairs={{0,2},{1,3},{2,0},{3,1},{4,6},{5,7},{6,4},{7,5},{8,10},{9,11},{10,... | collective-permute-start | bytes 2543624 | tf_op jit(solution)/shard_map/ppermute | solution.py:417
  130.8 23.3 %collective-permute-start.19 = (bf16[368,1152]{1,0:T(8,128)(2,1)S(1)}, bf16[368,1152]{1,0:T(8,128)(2,1)}, u32[]{:S(2)}, u32[]{:S(2)}) collective-permute-start(bf16[368,1152]{1,0:T(8,128)(2,1)S(1)} %add_convert_fusion.2.chip_ref), channel_id=1, source_target_pairs={{0,2},{1,3},{2,0},{3,1},{4,6},{5,7},{6,4},{7,5},{8,10},{9,11},{10,... | collective-permute-start | bytes 2543624 | tf_op jit(solution)/shard_map/ppermute | solution.py:417
  158.9 21.1 %collective-permute-start.24 = (bf16[368,1152]{1,0:T(8,128)(2,1)S(1)}, bf16[368,1152]{1,0:T(8,128)(2,1)S(1)}, u32[]{:S(2)}, u32[]{:S(2)}) collective-permute-start(bf16[368,1152]{1,0:T(8,128)(2,1)S(1)} %add_convert_fusion.1.chip_ref), channel_id=1, source_target_pairs={{0,2},{1,3},{2,0},{3,1},{4,6},{5,7},{6,4},{7,5},{8,10},{9,11},{10,... | collective-permute-start | bytes 2543624 | tf_op jit(solution)/shard_map/ppermute | solution.py:417
  206.9 26.6 %collective-permute-start.16 = (bf16[368,1152]{1,0:T(8,128)(2,1)}, bf16[368,1152]{1,0:T(8,128)(2,1)S(1)}, u32[]{:S(2)}, u32[]{:S(2)}) collective-permute-start(bf16[368,1152]{1,0:T(8,128)(2,1)} %copy-done.28), channel_id=1, source_target_pairs={{0,1},{1,0},{2,3},{3,2},{4,5},{5,4},{6,7},{7,6},{8,9},{9,8},{10,11... | collective-permute-start | bytes 2543624 | tf_op jit(solution)/shard_map/ppermute | solution.py:417
  207.4 27.9 %collective-permute-start.22 = (bf16[368,1152]{1,0:T(8,128)(2,1)}, bf16[368,1152]{1,0:T(8,128)(2,1)S(1)}, u32[]{:S(2)}, u32[]{:S(2)}) collective-permute-start(bf16[368,1152]{1,0:T(8,128)(2,1)} %copy-done.30), channel_id=1, source_target_pairs={{0,1},{1,0},{2,3},{3,2},{4,5},{5,4},{6,7},{7,6},{8,9},{9,8},{10,11... | collective-permute-start | bytes 2543624 | tf_op jit(solution)/shard_map/ppermute | solution.py:417
  209.1 21.3 %collective-permute-start.29 = (bf16[368,1152]{1,0:T(8,128)(2,1)S(1)}, bf16[368,1152]{1,0:T(8,128)(2,1)S(1)}, u32[]{:S(2)}, u32[]{:S(2)}) collective-permute-start(bf16[368,1152]{1,0:T(8,128)(2,1)S(1)} %add_convert_fusion.chip_ref), channel_id=1, source_target_pairs={{0,2},{1,3},{2,0},{3,1},{4,6},{5,7},{6,4},{7,5},{8,10},{9,11},{10,... | collective-permute-start | bytes 2543624 | tf_op jit(solution)/shard_map/ppermute | solution.py:417
  234.6 40.3 %collective-permute-start.17 = (bf16[184,1152]{1,0:T(8,128)(2,1)}, bf16[184,1152]{1,0:T(8,128)(2,1)}, u32[]{:S(2)}, u32[]{:S(2)}) collective-permute-start(bf16[184,1152]{1,0:T(8,128)(2,1)} %add_convert_fusion.9), channel_id=1, source_target_pairs={{0,2},{1,3},{2,0},{3,1},{4,6},{5,7},{6,4},{7,5},{8,10},{9,11},{10,... | collective-permute-start | bytes 1271816 | tf_op jit(solution)/shard_map/ppermute | solution.py:417
  236.4 38.5 %collective-permute-start.23 = (bf16[184,1152]{1,0:T(8,128)(2,1)}, bf16[184,1152]{1,0:T(8,128)(2,1)}, u32[]{:S(2)}, u32[]{:S(2)}) collective-permute-start(bf16[184,1152]{1,0:T(8,128)(2,1)} %add_convert_fusion.7), channel_id=1, source_target_pairs={{0,2},{1,3},{2,0},{3,1},{4,6},{5,7},{6,4},{7,5},{8,10},{9,11},{10,... | collective-permute-start | bytes 1271816 | tf_op jit(solution)/shard_map/ppermute | solution.py:417
  254.7 22.9 %collective-permute-start.27 = (bf16[184,1152]{1,0:T(8,128)(2,1)S(1)}, bf16[184,1152]{1,0:T(8,128)(2,1)S(1)}, u32[]{:S(2)}, u32[]{:S(2)}) collective-permute-start(bf16[184,1152]{1,0:T(8,128)(2,1)S(1)} %add_convert_fusion.5), channel_id=1, source_target_pairs={{0,2},{1,3},{2,0},{3,1},{4,6},{5,7},{6,4},{7,5},{8,10},{9,11},{10,... | collective-permute-start | bytes 1271816 | tf_op jit(solution)/shard_map/ppermute | solution.py:417
  271.0 32.5 %collective-permute-start.39 = (bf16[3,144,1152]{2,1,0:T(8,128)(2,1)S(1)}, bf16[3,144,1152]{2,1,0:T(8,128)(2,1)S(1)}, u32[]{:S(2)}, u32[]{:S(2)}) collective-permute-start(bf16[3,144,1152]{2,1,0:T(8,128)(2,1)S(1)} %pad_maximum_fusion.1), channel_id=1, source_target_pairs={{0,4},{4,0},{8,12},{12,8},{16,20},{20,16},{24,28},{28,24},{1,5},{5... | collective-permute-start | bytes 2985992 | tf_op jit(solution)/shard_map/ppermute | solution.py:420
  277.5 39.1 %collective-permute-start.38 = (bf16[144,1152]{1,0:T(8,128)(2,1)}, bf16[144,1152]{1,0:T(8,128)(2,1)}, u32[]{:S(2)}, u32[]{:S(2)}) collective-permute-start(bf16[144,1152]{1,0:T(8,128)(2,1)} %get-tuple-element.172), channel_id=1, source_target_pairs={{0,4},{4,0},{8,12},{12,8},{16,20},{20,16},{24,28},{28,24},{1,5},{5... | collective-permute-start | bytes 995336 | tf_op jit(solution)/shard_map/ppermute | solution.py:420
  285.6 21.5 %collective-permute-start.33 = (f32[6,1152]{1,0:T(8,128)S(1)}, f32[6,1152]{1,0:T(8,128)S(1)}, u32[]{:S(2)}, u32[]{:S(2)}) collective-permute-start(f32[6,1152]{1,0:T(8,128)S(1)} %maximum_add_fusion), channel_id=1, source_target_pairs={{0,1},{1,0},{2,3},{3,2},{4,5},{5,4},{6,7},{7,6},{8,9},{9,8},{10,11... | collective-permute-start | bytes 82952 | tf_op jit(solution)/shard_map/ppermute | solution.py:417
  304.9 22.0 %collective-permute-start.42 = (bf16[144,1152]{1,0:T(8,128)(2,1)S(1)}, bf16[144,1152]{1,0:T(8,128)(2,1)S(1)}, u32[]{:S(2)}, u32[]{:S(2)}) collective-permute-start(bf16[144,1152]{1,0:T(8,128)(2,1)S(1)} %get-tuple-element.170), channel_id=1, source_target_pairs={{0,16},{4,20},{8,24},{12,28},{16,0},{20,4},{24,8},{28,12},{1,17},{... | collective-permute-start | bytes 995336 | tf_op jit(solution)/shard_map/ppermute | solution.py:423
  305.0 22.0 %collective-permute-start.41 = (bf16[144,1152]{1,0:T(8,128)(2,1)S(1)}, bf16[144,1152]{1,0:T(8,128)(2,1)}, u32[]{:S(2)}, u32[]{:S(2)}) collective-permute-start(bf16[144,1152]{1,0:T(8,128)(2,1)S(1)} %get-tuple-element.171), channel_id=1, source_target_pairs={{0,24},{4,28},{8,0},{12,4},{16,8},{20,12},{24,16},{28,20},{1,25},{... | collective-permute-start | bytes 995336 | tf_op jit(solution)/shard_map/ppermute | solution.py:423
  305.9 22.7 %collective-permute-start.40 = (bf16[144,1152]{1,0:T(8,128)(2,1)S(1)}, bf16[144,1152]{1,0:T(8,128)(2,1)}, u32[]{:S(2)}, u32[]{:S(2)}) collective-permute-start(bf16[144,1152]{1,0:T(8,128)(2,1)S(1)} %get-tuple-element.169), channel_id=1, source_target_pairs={{0,8},{4,12},{8,16},{12,20},{16,24},{20,28},{24,0},{28,4},{1,9},{5... | collective-permute-start | bytes 995336 | tf_op jit(solution)/shard_map/ppermute | solution.py:423
  (77 other events, 760.0 us)
Sparse Core Ops, SparseCore 0:
  37.8 93.4 all-gather.1
  199.0 107.9 reduce-scatter.1
